TPU v7x, 32 devices: a whole 2x2x4 slice. The times are simulated.
32 devices in a mesh: dp: 8 (over z, core), group: 4 (over y, x).
Axes of the slice: x: 2, y: 2, z: 4, core: 2. Of those that a mesh axis runs over, the one named last changes fastest.
Arguments:
- tokens: bfloat16 [32768, 1024], P(('dp', 'group')), may hold values from -6 to 6
- cotangent: bfloat16 [32768, 1024], P(('dp', 'group')), may hold values from -6 to 6
- doc_ids: int32 [32768], P(('dp', 'group')), may hold values from -1 to 3, as said below
- master: float32 [12587008], P('group')
- moment_one: float32 [12587008], P('group'), may hold values from -2 to 2
- moment_two: float32 [12587008], P('group'), may hold values from 0.001 to 1
Outputs:
- mixed: bfloat16 [32768, 1024], P(('dp', 'group'))
- input_grad: bfloat16 [32768, 1024], P(('dp', 'group'))
- weight_grad: float32 [12587008], P('group')
- master_step: float32 [12587008], P('group')
- new_moment_one: float32 [12587008], P('group')
Inputs may be any that keep to these rules, and one draw needn't show every extreme that they name: `doc_ids`: each device's block of 1024 slots holds one to four sequences numbered 0, 1, ... in order, each of 16 tokens or more, followed by padding slots of -1 at its end; some device holds a single sequence of 1024 tokens and some device holds four.
All inputs are finite; a program needn't handle non-finite values.
Results may differ from a plain program's by a relative error of at most 0.012.
Values may be sent and summed in bfloat16 or wider, within the bound.
A program may use at most 384 MiB of HBM per device.

v0:
```python
import functools

import jax
import jax.numpy as jnp
from jax import lax
from jax.experimental import pallas as pl
from jax.experimental.pallas import tpu as pltpu
from jax.sharding import Mesh
from jax.sharding import PartitionSpec as P

HEADS = 16
EPS = 1e-05
FILL = -1e30
BETA_ONE = 0.9
BETA_TWO = 0.999
RATE = 0.001
ADAM_EPS = 1e-08
STEPS = 100.0
VMEM_MB = 60

f32 = jnp.float32
bf16 = jnp.bfloat16
ANY = pl.BlockSpec(memory_space=pl.ANY)


def params(limit=VMEM_MB):
    return pltpu.CompilerParams(vmem_limit_bytes=limit << 20)


def cost(flops, nbytes, trans=0):
    return pl.CostEstimate(flops=int(flops), bytes_accessed=int(nbytes), transcendentals=int(trans))


def sds(shape, dtype):
    return jax.ShapeDtypeStruct(shape, dtype)


def dot_nn(a, b):
    return jnp.dot(a, b, preferred_element_type=f32)


def dot_nt(a, b):
    return lax.dot_general(a, b, (((1,), (1,)), ((), ())), preferred_element_type=f32)


def dot_tn(a, b):
    return lax.dot_general(a, b, (((0,), (0,)), ((), ())), preferred_element_type=f32)


def pick(flag, a, b):
    return jnp.where(flag, a, b)


MESH = pl.DeviceIdType.MESH


def peer(*axes):
    return {a: 1 - lax.axis_index(a) for a in axes}


def greet(peers):
    barrier = pltpu.get_barrier_semaphore()
    for p in peers:
        pl.semaphore_signal(barrier, inc=1, device_id=p, device_id_type=MESH)
    pl.semaphore_wait(barrier, len(peers))


def member():
    return lax.axis_index("y") * 2 + lax.axis_index("x")


class Gather:
    COUNT = 11

    def __init__(self, own, oth, send, recv, base):
        rows = own.shape[0] // 4
        half = rows // 2
        x, y = lax.axis_index("x"), lax.axis_index("y")
        share = [y * 2 + x, y * 2 + 1 - x, (1 - y) * 2 + x, (1 - y) * 2 + 1 - x]
        self.rows = [pl.ds(pl.multiple_of(k * rows, 8), rows) for k in share]

        def move(i, k, off, count, dst, to):
            at = pl.ds(pl.multiple_of(share[k] * rows + off, 8), count)
            return pltpu.make_async_remote_copy(
                src_ref=own.at[at, :], dst_ref=dst.at[at, :],
                send_sem=send.at[base + i], recv_sem=recv.at[base + i], device_id=peer(to), device_id_type=MESH,
            )

        self.moves = [
            move(0, 0, 0, half, own, "x"),
            move(1, 0, half, half, own, "x"),
            move(2, 0, half, half, own, "y"),
            move(3, 0, 0, half, own, "y"),
            move(4, 0, 0, rows, oth, "core"),
            move(5, 1, 0, half, own, "y"),
            move(6, 2, half, half, own, "x"),
            move(7, 1, 0, rows, oth, "core"),
            move(8, 2, 0, rows, oth, "core"),
            move(9, 3, 0, half, oth, "core"),
            move(10, 3, half, half, oth, "core"),
        ]

    def begin(self):
        for i in (0, 2, 1, 3, 4):
            self.moves[i].start()

    def relay(self):
        self.moves[0].wait_recv()
        self.moves[5].start()
        self.moves[2].wait_recv()
        self.moves[6].start()

    def forward(self):
        self.moves[1].wait_recv()
        self.moves[7].start()
        self.moves[3].wait_recv()
        self.moves[8].start()

    def close(self):
        self.moves[5].wait_recv()
        self.moves[9].start()
        self.moves[6].wait_recv()
        self.moves[10].start()

    def arrive(self, *which):
        for i in which:
            self.moves[i].wait_recv()

    def sent(self):
        for m in self.moves:
            m.wait_send()

    def finish(self):
        self.close()
        self.arrive(4, 7, 8, 9, 10)
        self.sent()


def hand_over(src, dst, send, recv):
    return pltpu.make_async_remote_copy(
        src_ref=src, dst_ref=dst, send_sem=send, recv_sem=recv, device_id=peer("core"), device_id_type=MESH
    )


def add_up(dst, a, b):
    rows, cols = dst.shape
    step = max(8, 16384 // cols)

    @pl.loop(0, rows // step)
    def _(i):
        at = pl.ds(pl.multiple_of(i * step, 8), step)
        dst[at, :] = (a[at, :].astype(f32) + b[at, :].astype(f32)).astype(bf16)


class Fold:
    def __init__(self, source, mine, inbox, cross, stage, total, red, theirs, keep, send, recv, base):
        self.pieces = len(mine)
        self.out = [pltpu.make_async_copy(total.at[s], red.at[s], keep.at[s]) for s in range(self.pieces)]
        z = lax.axis_index("z")
        self.end = (z == 0) | (z == 3)
        self.mid = (z == 1) | (z == 2)
        near, far = self.peers()
        self.mine, self.inbox, self.across, self.stage, self.total = mine, inbox, cross, stage, total

        def move(s, kind, src, dst, to):
            i = base + 4 * s + kind
            return pltpu.make_async_remote_copy(
                src_ref=src, dst_ref=dst, send_sem=send.at[i], recv_sem=recv.at[i], device_id=to, device_id_type=MESH
            )

        every = range(self.pieces)
        self.fold = [move(s, 0, source[s], inbox.at[s], near) for s in every]
        self.cross = [move(s, 1, stage.at[s], cross.at[s], far) for s in every]
        self.unfold = [move(s, 2, total.at[s], total.at[s], near) for s in every]
        self.core = [move(s, 3, total.at[s], theirs.at[s], peer("core")) for s in every]

    @staticmethod
    def peers():
        z = lax.axis_index("z")
        return [{"z": z + 1 - 2 * (z % 2)}, {"z": 3 - z}]

    def begin(self, s):
        pl.when(self.end)(self.fold[s].start)

    def inner(self, s):
        @pl.when(self.mid)
        def _():
            self.fold[s].wait_recv()
            add_up(self.stage.at[s], self.mine[s], self.inbox.at[s])
            self.cross[s].start()

    def outer(self, s):
        @pl.when(self.mid)
        def _():
            self.cross[s].wait_recv()
            add_up(self.total.at[s], self.stage.at[s], self.across.at[s])
            self.unfold[s].start()
            self.core[s].start()
            self.out[s].start()

    def land(self, s):
        @pl.when(self.end)
        def _():
            self.unfold[s].wait_recv()
            self.core[s].start()
            self.out[s].start()

    def finish(self):
        @pl.when(self.end)
        def _():
            for m in self.fold:
                m.wait_send()

        @pl.when(self.mid)
        def _():
            for m in self.cross + self.unfold:
                m.wait_send()

        for m in self.core + self.out:
            m.wait()


def pieces_of(ref):
    return [ref.at[i] for i in range(ref.shape[0])]


def fold_scratch(pieces, rows, cols):
    return [pltpu.VMEM((pieces, rows, cols), bf16)] * 4


class Scatter:
    def __init__(self, source, held, far, near, mid, total, send, recv, base, out=None, keep=None):
        pieces, rows, _ = held.shape
        self.out = [] if out is None else [pltpu.make_async_copy(total.at[s], out.at[s], keep.at[s]) for s in range(pieces)]
        block = rows // 4
        half = block // 2
        x, y = lax.axis_index("x"), lax.axis_index("y")
        me, over_x, over_y, both = y * 2 + x, y * 2 + 1 - x, (1 - y) * 2 + x, (1 - y) * 2 + 1 - x
        self.pieces, self.held, self.far, self.near, self.mid, self.total, self.half = pieces, held, far, near, mid, total, half

        def at(share, part):
            return pl.ds(pl.multiple_of(share * block + part * half, half), half)

        def move(i, src, dst, to):
            return pltpu.make_async_remote_copy(
                src_ref=src, dst_ref=dst, send_sem=send.at[base + i], recv_sem=recv.at[base + i],
                device_id=peer(to), device_id_type=MESH,
            )

        self.first, self.second = [], []
        for s in range(pieces):
            b = 6 * s
            self.first.append([
                move(b, source.at[s, at(over_x, 0), :], far.at[s, 0], "x"),
                move(b + 1, source.at[s, at(both, 0), :], far.at[s, 1], "x"),
                move(b + 2, source.at[s, at(over_y, 1), :], far.at[s, 2], "y"),
                move(b + 3, source.at[s, at(both, 1), :], far.at[s, 3], "y"),
            ])
            self.second.append([move(b + 4, mid.at[s, 1], near.at[s, 0], "y"), move(b + 5, mid.at[s, 3], near.at[s, 1], "x")])
        self.keep = [at(me, 0), at(over_y, 0), at(me, 1), at(over_x, 1)]

    def begin(self, s):
        for k in (1, 3, 0, 2):
            self.first[s][k].start()

    def turn(self, s):
        for k in (1, 3, 0, 2):
            self.first[s][k].wait_recv()
            add_up(self.mid.at[s, k], self.held.at[s, self.keep[k], :], self.far.at[s, k])
            if k in (1, 3):
                self.second[s][k // 2].start()

    def close(self, s):
        for part in range(2):
            self.second[s][part].wait_recv()
            at = pl.ds(part * self.half, self.half)
            add_up(self.total.at[s, at, :], self.mid.at[s, 2 * part], self.near.at[s, part])
        if self.out:
            self.out[s].start()

    def finish(self):
        for s in range(self.pieces):
            for m in self.first[s] + self.second[s]:
                m.wait_send()
        for m in self.out:
            m.wait()


def scatter_scratch(pieces, rows, cols):
    half = rows // 8
    four = pltpu.VMEM((pieces, 4, half, cols), bf16)
    return [pltpu.VMEM((pieces, rows, cols), bf16), four, pltpu.VMEM((pieces, 2, half, cols), bf16), four]


def swap_core(v):
    return lax.ppermute(v, "core", [(0, 1), (1, 0)])


def comm_params(cid, limit=VMEM_MB):
    if cid is None:
        return params(limit)
    return pltpu.CompilerParams(vmem_limit_bytes=limit << 20, collective_id=cid, has_side_effects=True)


def dma(count):
    return pltpu.SemaphoreType.DMA((count,))


def gain_row(norms, r, d):
    nb = d // 128
    return jnp.concatenate([norms[r * nb + i : r * nb + i + 1, :] for i in range(nb)], axis=1)


def layer_norm_parts(v):
    centre = v - jnp.mean(v, axis=-1, keepdims=True)
    r = lax.rsqrt(jnp.mean(centre * centre, axis=-1, keepdims=True) + EPS)
    return centre * r, r


def layer_norm_back(v, gain, dz):
    xhat, r = layer_norm_parts(v)
    dg = jnp.sum(dz * xhat, axis=0, keepdims=True)
    db = jnp.sum(dz, axis=0, keepdims=True)
    t = dz * gain
    dv = r * (t - jnp.mean(t, axis=-1, keepdims=True) - xhat * jnp.mean(t * xhat, axis=-1, keepdims=True))
    return dv, dg, db


def unpack_kernel(dims, m_qkv, m_out, m_norm, own_qkv, own_out, norm):
    n, d = dims
    core = lax.axis_index("core")
    nb = d // 128
    half = nb // 2
    rows = own_qkv.shape[0]

    def put(ref, own, dst, lo, stride):
        own[:, dst : dst + 128] = ref[pl.ds(lo + core * half, rows, stride=stride), :].astype(bf16)

    for part in range(3):
        for w in range(half):
            put(m_qkv, own_qkv, (part * half + w) * 128, part * nb + w, 3 * nb)
    for w in range(half):
        put(m_out, own_out, w * 128, w, nb)
    norm[...] = m_norm[...].astype(bf16).astype(f32)


def group_index(n):
    return lax.axis_index(("y", "x"))


def unpack_first(lanes, n, d, ff):
    rows = d // n
    nb = d // 128
    r1, r2, r3, r4 = rows * 3 * nb, rows * nb, rows * ff // 128, ff // n * nb
    steps = 4 if n == 4 else 2
    sr = rows // steps
    me = lambda: group_index(n)
    return pl.pallas_call(
        functools.partial(unpack_kernel, (n, d)),
        grid=(steps,),
        out_shape=[sds((d, 3 * d // 2), bf16), sds((d, d // 2), bf16), sds((8, 128), f32)],
        in_specs=[
            pl.BlockSpec((r1 // steps, 128), lambda i: (i, 0)),
            pl.BlockSpec((r2 // steps, 128), lambda i: (r1 // (r2 // steps) + i, 0)),
            pl.BlockSpec((8, 128), lambda i: ((r1 + r2 + r3 + r4) // 8, 0)),
        ],
        out_specs=[
            pl.BlockSpec((sr, 3 * d // 2), lambda i: (me() * steps + i, 0)),
            pl.BlockSpec((sr, d // 2), lambda i: (me() * steps + i, 0)),
            pl.BlockSpec((8, 128), lambda i: (0, 0)),
        ],
        compiler_params=params(),
        name="unpack",
    )(lanes, lanes, lanes)


UNPACK_STEPS = 8


def qkv_kernel(cfg, tok, norm_share, m_in, m_back, w_own_in, w_oth_in, o_own_in, o_oth_in, *refs):
    n, comm = cfg
    (a_out, qkv, own_in, own_bk, w_own, w_oth, o_own, o_oth, norms_out, norms, w, toks, acc, lsem, send, recv) = refs
    if not comm:
        w_own, w_oth = w_own_in, w_oth_in
    t, d = toks.shape
    step = pl.program_id(0)
    nb = d // 128
    half = 3 * d // 2
    share = d // n
    tm = min(256, t)
    tok_copy = pltpu.make_async_copy(tok, toks, lsem.at[0])

    if comm:
        me = member()
        near = [peer("x"), peer("y"), peer("x", "y")]
        mine = pl.ds(pl.multiple_of(me * 8, 8), 8)
        notes = [
            pltpu.make_async_remote_copy(
                src_ref=norm_share, dst_ref=norms.at[mine, :], send_sem=send.at[22 + i], recv_sem=recv.at[22 + i],
                device_id=p, device_id_type=MESH,
            )
            for i, p in enumerate(near)
        ]
        first = Gather(w_own, w_oth, send, recv, 0)
        second = Gather(o_own, o_oth, send, recv, 11)
        rows = first.rows
    else:
        rows = [pl.ds(k * share, share) for k in range(n)]

    @pl.when(step == 0)
    def _():
        tok_copy.start()
        if comm:
            greet(near + [peer("core")])
            for m in notes:
                m.start()
            first.begin()
            norms[mine, :] = norm_share[...]

    @pl.when(step < UNPACK_STEPS)
    def _():
        core = lax.axis_index("core")
        rows_in = own_in.shape[0]
        hs = own_in.shape[1] // n
        stride = m_in.shape[0] // rows_in
        for j in range(n):
            for q in range(hs // 128):
                lo = (2 * hs * j) // 128 + q + core * (hs // 128)
                at = hs * j + q * 128
                own_in[:, at : at + 128] = m_in[pl.ds(lo, rows_in, stride=stride), :].astype(bf16)
        for q in range(nb):
            own_bk[:, q * 128 : (q + 1) * 128] = m_back[pl.ds(q, own_bk.shape[0], stride=nb), :].astype(bf16)

    def load(*which):
        cps = []
        for k in which:
            cps.append(pltpu.make_async_copy(w_own.at[rows[k], :], w.at[k, :, pl.ds(0, half)], lsem.at[1 + 2 * k]))
            cps.append(pltpu.make_async_copy(w_oth.at[rows[k], :], w.at[k, :, pl.ds(half, half)], lsem.at[2 + 2 * k]))
        for cp in cps:
            cp.start()
        for cp in cps:
            cp.wait()

    def product(at, *which):
        return sum(dot_nn(a_out[at, cols_of(k)], w[k]) for k in which)

    def cols_of(k):
        if comm:
            return rows[k]
        return slice(k * share, (k + 1) * share)

    def each_block(fn):
        @pl.loop(0, t // tm)
        def _(i):
            fn(pl.ds(pl.multiple_of(i * tm, tm), tm))

    @pl.when(step == UNPACK_STEPS)
    def _():
        if comm:
            for m in notes:
                m.wait()
            first.relay()
            second.begin()
        else:
            norms[...] = norm_share[...]
        norms_out[...] = norms[...]
        tok_copy.wait()
        gain, bias = gain_row(norms, 0, d), gain_row(norms, 1, d)

        def norm(at):
            xhat, _ = layer_norm_parts(toks[at, :].astype(f32))
            a_out[at, :] = (xhat * gain + bias).astype(bf16)

        each_block(norm)
        if comm:
            first.arrive(4)
        load(0)

        def start(at):
            acc[at, :] = product(at, 0)

        each_block(start)

    @pl.when(step == UNPACK_STEPS + 1)
    def _():
        if comm:
            first.forward()
            first.arrive(7, 8)
        load(*range(1, n - 1))

        def more(at):
            acc[at, :] += product(at, *range(1, n - 1))

        each_block(more)

    @pl.when(step == UNPACK_STEPS + 2)
    def _():
        if comm:
            first.close()
            second.relay()
            first.arrive(9, 10)
        load(n - 1)
        scale = (d // HEADS) ** (-0.5)
        q = d // 2

        def last(at):
            total = acc[at, :] + product(at, n - 1)
            for o in (0, half):
                qkv[at, o : o + q] = (total[:, o : o + q].astype(bf16).astype(f32) * scale).astype(bf16)
                qkv[at, o + q : o + half] = total[:, o + q : o + half].astype(bf16)

        each_block(last)
        if comm:
            second.forward()
            second.finish()
            first.sent()


def project_qkv(lanes, tok, norm_share, w, o, n, ff, comm):
    t, d = tok.shape
    rows = d // n
    nb = d // 128
    hs = ff // n // 2
    r_in, r_bk = rows * ff // 128, ff // n * nb
    at_in, at_bk = rows * 4 * nb, rows * 4 * nb + r_in
    b_in, b_bk = r_in // UNPACK_STEPS, hs * nb // UNPACK_STEPS
    assert at_in % b_in == 0 and at_bk % b_bk == 0
    up = lambda i: jnp.minimum(i, UNPACK_STEPS - 1)
    me = lambda: group_index(n)
    whole = lambda s: pl.BlockSpec(s, lambda i: (0, 0))
    half = 3 * d // 2
    shapes = [sds((t, d), bf16), sds((t, 3 * d), bf16), sds((d, ff // 2), bf16), sds((ff // 2, d), bf16),
              sds((d, half), bf16), sds((d, half), bf16), sds((d, d // 2), bf16), sds((d, d // 2), bf16), sds((4 * nb, 128), f32)]
    w_args = [w, norm_share, o, norm_share] if comm else [w[0], w[1], o[0], o[1]]
    outs = pl.pallas_call(
        functools.partial(qkv_kernel, (n, comm)),
        grid=(UNPACK_STEPS + 3,),
        out_shape=shapes,
        in_specs=[
            ANY, whole(norm_share.shape),
            pl.BlockSpec((b_in, 128), lambda i: (at_in // b_in + up(i), 0)),
            pl.BlockSpec((b_bk, 128), lambda i: (at_bk // b_bk + lax.axis_index("core") * UNPACK_STEPS + up(i), 0)),
            ANY, ANY, ANY, ANY,
        ],
        out_specs=[
            whole((t, d)), whole((t, 3 * d)),
            pl.BlockSpec((rows // UNPACK_STEPS, ff // 2), lambda i: (me() * UNPACK_STEPS + up(i), 0)),
            pl.BlockSpec((hs // UNPACK_STEPS, d), lambda i: (me() * UNPACK_STEPS + up(i), 0)),
            ANY, ANY, ANY, ANY, whole((4 * nb, 128)),
        ],
        scratch_shapes=[pltpu.VMEM((4 * nb, 128), f32), pltpu.VMEM((n, rows, 3 * d), bf16), pltpu.VMEM((t, d), bf16),
                        pltpu.VMEM((t, 3 * d), f32), dma(1 + 2 * n), dma(25), dma(25)],
        input_output_aliases={4: 4, 6: 6},
        compiler_params=comm_params(1 if comm else None),
        cost_estimate=cost(2 * t * d * 3 * d, 40e6),
        name="qkv",
    )(tok, norm_share, lanes, lanes, *w_args)
    if comm:
        return outs
    return [*outs[:4], w[0], w[1], o[0], o[1], outs[8]]


QB = 256


def fill_bias(bias, doc_row, doc_col):
    t = bias.shape[0]
    for r in range(0, t, QB):
        key = r + lax.broadcasted_iota(jnp.int32, (QB, t), 0)
        query = lax.broadcasted_iota(jnp.int32, (QB, t), 1)
        ok = (doc_col[r : r + QB, :] == doc_row[...]) & (key <= query)
        bias[r : r + QB, :] = jnp.where(ok, 0.0, FILL)


def head_lanes(v, h, hd):
    lane = lax.broadcasted_iota(jnp.int32, v.shape, 1)
    return jnp.where((lane >= h * hd) & (lane < (h + 1) * hd), v, jnp.zeros_like(v))


def attend_kernel(cfg, q, k, v, doc_row, doc_col, w_own_in, a_one, d_out, out, lse, w_own, w_oth, a_p, d_p, bias, send, recv):
    hd, comm = cfg
    step = pl.program_id(0)
    last = pl.num_programs(0) - 1
    if comm:
        gather = Gather(w_own, w_oth, send, recv, 0)
        swaps = [hand_over(a_one, a_p, send.at[11], recv.at[11]), hand_over(d_out, d_p, send.at[12], recv.at[12])]

        @pl.when(step == 0)
        def _():
            greet([peer("x"), peer("y"), peer("core")])
            gather.begin()
            for s in swaps:
                s.start()

        @pl.when(step == 4)
        def _():
            gather.relay()

        @pl.when(step == 6)
        def _():
            gather.forward()

    @pl.when(step == 0)
    def _():
        fill_bias(bias, doc_row, doc_col)

    t = q.shape[0]
    vt = v[...].T
    per = 128 // hd
    qs = [head_lanes(q[...], h, hd) for h in range(per)]
    for i in range(t // QB):
        n = (i + 1) * QB
        cols = slice(i * QB, n)
        outs = []
        for h in range(per):
            s = dot_nt(k[:n, :], qs[h][cols, :]) + bias[:n, cols]
            top = jnp.max(s, axis=0, keepdims=True)
            e = jnp.exp(s - top)
            total = jnp.sum(e, axis=0, keepdims=True)
            lse[0, h : h + 1, cols] = top + jnp.log(total)
            o = dot_nn(vt[h * hd : (h + 1) * hd, :n], e.astype(bf16))
            outs.append(o * (1.0 / total))
        out[cols, :] = jnp.concatenate(outs, axis=0).T.astype(bf16)

    if comm:

        @pl.when(step == last)
        def _():
            gather.finish()
            for s in swaps:
                s.wait()


def head_column(d, part):
    pairs = d // 256
    return lambda p: (0, (p // pairs) * 3 * pairs + part * pairs + p % pairs)


def attend(qkv, doc_row, doc_col, w_own, a_one, d_out, d, comm):
    t = qkv.shape[0]
    pairs = d // 128
    hd = d // HEADS
    per = 128 // hd
    col = lambda part: pl.BlockSpec((t, 128), head_column(d, part))
    outs = pl.pallas_call(
        functools.partial(attend_kernel, (hd, comm)),
        grid=(pairs,),
        out_shape=[sds((t, d), bf16), sds((pairs, per, t), f32), sds(w_own.shape, bf16), sds(w_own.shape, bf16),
                   sds((t, d), bf16), sds((t, d), bf16)],
        in_specs=[col(0), col(1), col(2), pl.BlockSpec((1, t), lambda p: (0, 0)), pl.BlockSpec((t, 1), lambda p: (0, 0)),
                  ANY, ANY, ANY],
        out_specs=[pl.BlockSpec((t, 128), lambda p: (0, p)), pl.BlockSpec((1, per, t), lambda p: (p, 0, 0)), ANY, ANY, ANY, ANY],
        scratch_shapes=[pltpu.VMEM((t, t), f32), dma(13), dma(13)],
        input_output_aliases={5: 2},
        compiler_params=comm_params(2 if comm else None),
        cost_estimate=cost(8 * t * t * d, 10e6, t * t * HEADS),
        name="attend",
    )(qkv, qkv, qkv, doc_row, doc_col, w_own, a_one, d_out)
    if comm:
        return outs
    full, oth = spread(w_own)
    return outs[0], outs[1], full, oth, swap_core(a_one), swap_core(d_out)


def spread(own):
    n = lax.axis_size("y") * lax.axis_size("x")
    rows = own.shape[0] // n
    mine = lax.dynamic_slice_in_dim(own, lax.axis_index(("y", "x")) * rows, rows, 0)
    full = lax.all_gather(mine, ("y", "x"), axis=0, tiled=True)
    return full, swap_core(full)


def attend_back_kernel(cfg, q, k, v, dout, att, lse, doc_row, doc_col, part_sum, g_in, dq, dk, dv, sent, red, red_p, part_in, *refs):
    hd, comm = cfg
    bias, dk_acc, dv_acc, stage, lsem, send, recv = refs[:7]
    step = pl.program_id(0)
    pairs = stage.shape[0] // 3

    def hand(p, part):
        wide = 128 * pairs
        cols = pl.ds(pl.multiple_of(part * wide + p * 128, 128), 128)
        i = p * 3 + part
        return hand_over(stage.at[i], sent.at[:, cols], send.at[i], recv.at[i])

    if comm:

        base = 3 * pairs
        mine, keep, held, far, near, mid, total, keep_in = refs[7], refs[12], *refs[13:19]
        fold = Fold(pieces_of(part_sum), pieces_of(mine), *refs[8:12], red, red_p, keep, send, recv, base)
        scat = Scatter(g_in, held, far, near, mid, total, send, recv, base + 4 * PIECES, part_in, keep_in)
        acts = (scat.begin, scat.turn, scat.close, fold.inner, fold.outer, fold.land)

        @pl.when(step == 0)
        def _():
            loads = [pltpu.make_async_copy(part_sum, mine, lsem.at[0]), pltpu.make_async_copy(g_in, held, lsem.at[1])]
            for cp in loads:
                cp.start()
            greet([peer("core"), peer("x"), peer("y")] + Fold.peers())
            run_plan(acts, BACK_PLAN[0])
            for s in range(PIECES):
                fold.begin(s)
            for cp in loads:
                cp.wait()

        @pl.when((step > 0) & (step <= pairs))
        def _():
            for part in range(3):
                hand(step - 1, part).start()

    @pl.when(step == 0)
    def _():
        fill_bias(bias, doc_row, doc_col)

    if comm:
        for at, codes in enumerate(BACK_PLAN[:-1]):
            if codes and at > 0:
                pl.when(step == at)(functools.partial(run_plan, acts, codes))

    t = q.shape[0]
    per = 128 // hd
    scale = hd ** (-0.5)
    kt = k[...].T
    prod = (dout[...].astype(f32) * att[...].astype(f32)).T
    inner = [jnp.sum(prod[h * hd : (h + 1) * hd, :], axis=0, keepdims=True) for h in range(per)]
    qs = [head_lanes(q[...], h, hd) for h in range(per)]
    ds_ = [head_lanes(dout[...], h, hd) for h in range(per)]
    dk_acc[...] = jnp.zeros_like(dk_acc)
    dv_acc[...] = jnp.zeros_like(dv_acc)
    for i in range(t // QB):
        n = (i + 1) * QB
        cols = slice(i * QB, n)
        dqs = []
        for h in range(per):
            qh, dh = qs[h][cols, :], ds_[h][cols, :]
            s = dot_nt(k[:n, :], qh) + bias[:n, cols]
            p = jnp.exp(s - lse[0, h : h + 1, cols])
            dp = dot_nt(v[:n, :], dh)
            g = (p * (dp - inner[h][:, cols])).astype(bf16)
            dv_acc[:n, :] += dot_nn(p.astype(bf16), dh)
            dk_acc[:n, :] += dot_nn(g, qh)
            dqs.append(dot_nn(kt[h * hd : (h + 1) * hd, :n], g))
        dq[cols, :] = (jnp.concatenate(dqs, axis=0).T * scale).astype(bf16)
    dk[...] = dk_acc[...].astype(bf16)
    dv[...] = dv_acc[...].astype(bf16)

    if comm:

        @pl.when(step < pairs)
        def _():
            stage[step * 3] = dq[...]
            stage[step * 3 + 1] = dk[...]
            stage[step * 3 + 2] = dv[...]

        @pl.when(step == 2 * pairs - 1)
        def _():
            for p in range(pairs):
                for part in range(3):
                    hand(p, part).wait()
            run_plan(acts, BACK_PLAN[-1])
            fold.finish()
            scat.finish()


def run_plan(acts, codes):
    for code in codes:
        acts[code // 10](code % 10)


FEED_PLAN = (
    (0, 1),
    (),
    (10, 2),
    (11, 3, 20),
    (12, 4),
    (21, 13, 5),
    (22,),
    (14, 6, 23),
    (15, 7, 24),
    (16,),
    (25,),
    (17, 26),
    (),
    (27,),
    (),
    (),
    (),
)
BACK_PLAN = (
    (0, 1, 2),
    (),
    (10, 3, 11, 4, 30, 31),
    (12, 5, 20, 32, 33, 40),
    (13, 6, 21, 34, 35, 41, 42),
    (14, 7, 22, 36, 37, 43, 44, 50),
    (15, 23, 45, 51, 52, 16, 46),
    (17, 24, 47, 53, 54, 25),
    (26, 27, 55, 56, 57),
)
LAST_PLAN = (
    (),
    (0,),
    (1,),
    (30,),
    (10, 2, 31),
    (11, 3, 32, 40),
    (20, 33, 41),
    (12, 4, 34, 42),
    (21, 35, 43, 50),
    (13, 5, 22, 36, 44, 45, 37, 51),
    (14, 6, 23, 60, 46, 52, 53),
    (15, 7, 24, 61, 62, 70, 47, 54),
    (16, 25, 63, 64, 71, 55),
    (17, 26, 65, 72, 73, 66, 56, 90),
    (27, 67, 74, 75, 80, 91),
    (76, 81, 57, 92),
    (77, 93, 82, 94, 83, 95, 84, 85, 86, 87),
)
PIECES = 8


def attend_back(qkv, dout, att, lse, doc_row, doc_col, part_sum, g_in, d, n, comm):
    t = qkv.shape[0]
    pairs = d // 128
    half = pairs // 2
    hd = d // HEADS
    per = 128 // hd
    turn = lambda p: (p + half) % pairs
    part_in = (g_in.shape[0], g_in.shape[1] // n, g_in.shape[2])
    col = lambda part: pl.BlockSpec((t, 128), lambda p: head_column(d, part)(turn(p)))
    one = pl.BlockSpec((t, 128), lambda p: (0, turn(p)))
    sems = 3 * half + 10 * PIECES
    extra = []
    if comm:
        extra = [pltpu.VMEM(part_sum.shape, bf16)] + fold_scratch(*part_sum.shape) + [dma(PIECES)]
        extra += scatter_scratch(*g_in.shape) + [pltpu.VMEM(part_in, bf16), dma(PIECES)]
    outs = pl.pallas_call(
        functools.partial(attend_back_kernel, (hd, comm)),
        grid=(pairs,),
        out_shape=[sds((t, d), bf16)] * 3 + [sds((t, 3 * d // 2), bf16)] + [sds(part_sum.shape, bf16)] * 2 + [sds(part_in, bf16)],
        in_specs=[col(0), col(1), col(2), one, one, pl.BlockSpec((1, per, t), lambda p: (turn(p), 0, 0)),
                  pl.BlockSpec((1, t), lambda p: (0, 0)), pl.BlockSpec((t, 1), lambda p: (0, 0)), ANY, ANY],
        out_specs=[one, one, one, ANY, ANY, ANY, ANY],
        scratch_shapes=[pltpu.VMEM((t, t), f32), pltpu.VMEM((t, 128), f32), pltpu.VMEM((t, 128), f32),
                        pltpu.VMEM((3 * half, t, 128), bf16), dma(2), dma(sems), dma(sems)] + extra,
        compiler_params=comm_params(6 if comm else None),
        cost_estimate=cost(20 * t * t * d, 16e6, t * t * HEADS),
        name="attend_back",
    )(qkv, qkv, qkv, dout, att, lse, doc_row, doc_col, part_sum, g_in)
    if comm:
        return outs[0], outs[1], outs[2], outs[3], (outs[4], outs[5]), outs[6]
    sent = swap_core(jnp.concatenate([g[:, d // 2 :] for g in outs[:3]], axis=1))
    return outs[0], outs[1], outs[2], sent, both_halves(part_sum), scatter_pieces(g_in)


def both_halves(part_sum):
    full = lax.psum(part_sum.astype(f32), "z").astype(bf16)
    return full, swap_core(full)


def middle_kernel(cfg, att_rows, tok, norms, o_own, o_oth, w_own, w_oth, att_all, bk_own_in, d_out, d_out_p, *refs):
    d, tm, blk, comm = cfg
    (resid, a_two_out, hidden, slope, bk_own, bk_oth, att_p, grad, w, a_two, stage, theirs, douts, lsem, send, recv) = refs
    step = pl.program_id(0)
    last = pl.num_programs(0) - 1
    t = a_two.shape[0]
    pro = t // tm
    half = d // 2
    nb = theirs.shape[0]
    core = lax.axis_index("core")
    loads = [pltpu.make_async_copy(v, douts.at[i], lsem.at[2 + i]) for i, v in enumerate((d_out, d_out_p))]

    def hand(j):
        return hand_over(stage.at[j], theirs.at[j], send.at[12 + j], recv.at[12 + j])

    if comm:
        gather = Gather(bk_own, bk_oth, send, recv, 0)
        swap = hand_over(att_all, att_p, send.at[11], recv.at[11])

        @pl.when(step == 0)
        def _():
            greet([peer("x"), peer("y"), peer("core")])
            gather.begin()
            swap.start()

        @pl.when(step == pro + 4)
        def _():
            gather.relay()

        @pl.when((step > pro) & (step <= pro + nb))
        def _():
            hand(step - pro - 1).start()

    @pl.when(step == 0)
    def _():
        lo = pl.multiple_of(core * half, half)
        hi = pl.multiple_of((1 - core) * half, half)
        cps = [
            pltpu.make_async_copy(o_own, w.at[:, pl.ds(lo, half)], lsem.at[0]),
            pltpu.make_async_copy(o_oth, w.at[:, pl.ds(hi, half)], lsem.at[1]),
        ]
        for cp in cps + loads:
            cp.start()
        for cp in cps:
            cp.wait()

    @pl.when(step < pro)
    def _():
        lo = pl.multiple_of(core * half, half)
        hi = pl.multiple_of((1 - core) * half, half)
        y = dot_nn(att_rows[:, :half], w[pl.ds(lo, half), :]) + dot_nn(att_rows[:, half:], w[pl.ds(hi, half), :])
        r = tok[...].astype(f32) + y
        resid[...] = r
        xhat, _ = layer_norm_parts(r)
        a = (xhat * gain_row(norms, 2, d) + gain_row(norms, 3, d)).astype(bf16)
        a_two_out[...] = a
        a_two[pl.ds(pl.multiple_of(step * tm, tm), tm), :] = a

    @pl.when((step >= pro) & (step < pro + 2 * nb))
    def _():
        pre = dot_nn(a_two[...], pick(step < pro + nb, w_oth[...], w_own[...]))
        cdf = 0.5 + 0.5 * lax.erf(pre * (0.5**0.5))
        pdf = jnp.exp(-0.5 * pre * pre) * 0.3989422804014327
        h = (pre * cdf).astype(bf16)
        hidden[...] = h
        slope[...] = (cdf + pre * pdf).astype(bf16)
        stage[step - pro] = h

    @pl.when(step == pro + 2 * nb)
    def _():
        for cp in loads:
            cp.wait()

    if comm:
        for j in range(nb):

            @pl.when(step == pro + 2 * nb + j)
            def _():
                hand(j).wait_recv()

        @pl.when(step == pro + 2 * nb)
        def _():
            gather.forward()

    @pl.when(step >= pro + 2 * nb)
    def _():
        j = step - pro - 2 * nb
        g = dot_tn(stage[nb + j], douts[0])
        if comm:
            g = g + dot_tn(theirs[j], douts[1])
        store_columns(grad, g)

    if comm:

        @pl.when(step == last)
        def _():
            gather.finish()
            swap.wait()
            for j in range(nb):
                hand(j).wait_send()


def store_columns(ref, g):
    wide = ref.shape[2]
    for p in range(ref.shape[0]):
        ref[p] = g[:, p * wide : (p + 1) * wide].astype(bf16)


def middle(att, tok, norms, o_own, o_oth, w_own, w_oth, bk_own, d_out, d_out_p, comm, tm=256, blk=512):
    t, d = tok.shape
    wide = w_own.shape[1]
    pro, nb = t // tm, wide // blk
    rowi = lambda i: jnp.minimum(i, pro - 1)
    oth = lambda i: jnp.clip(i - pro, 0, nb - 1)
    own = lambda i: jnp.clip(i - pro - nb, 0, nb - 1)
    both = lambda i: jnp.where(i < pro + nb, nb + oth(i), own(i))
    rows = lambda wd: pl.BlockSpec((tm, wd), lambda i: (rowi(i), 0))
    part = lambda count: pltpu.VMEM((count, t, blk), bf16)
    outs = pl.pallas_call(
        functools.partial(middle_kernel, (d, tm, blk, comm)),
        grid=(pro + 3 * nb,),
        out_shape=[sds((t, d), f32), sds((t, d), bf16), sds((t, 2 * wide), bf16), sds((t, 2 * wide), bf16),
                   sds(bk_own.shape, bf16), sds(bk_own.shape, bf16), sds((t, d), bf16), sds((PIECES, wide, d // PIECES), bf16)],
        in_specs=[rows(d), rows(d), pl.BlockSpec(norms.shape, lambda i: (0, 0)), ANY, ANY,
                  pl.BlockSpec((d, blk), lambda i: (0, own(i))), pl.BlockSpec((d, blk), lambda i: (0, oth(i))), ANY, ANY, ANY, ANY],
        out_specs=[rows(d), rows(d), pl.BlockSpec((t, blk), lambda i: (0, both(i))), pl.BlockSpec((t, blk), lambda i: (0, both(i))),
                   ANY, ANY, ANY, pl.BlockSpec((PIECES, blk, d // PIECES), lambda i: (0, jnp.maximum(i - pro - 2 * nb, 0), 0))],
        scratch_shapes=[pltpu.VMEM((d, d), bf16), pltpu.VMEM((t, d), bf16), part(2 * nb), part(nb), pltpu.VMEM((2, t, d), bf16),
                        dma(4), dma(12 + nb), dma(12 + nb)],
        input_output_aliases={8: 4},
        compiler_params=comm_params(3 if comm else None),
        cost_estimate=cost(2 * t * d * d + 8 * t * d * wide, 60e6, 4 * t * wide),
        name="middle",
    )(att, tok, norms, o_own, o_oth, w_own, w_oth, att, bk_own, d_out, d_out_p)
    if comm:
        return outs
    full, other = spread(bk_own)
    hid_p = swap_core(outs[2][:, wide:])
    grad = (dot_tn(outs[2][:, :wide], d_out) + dot_tn(hid_p, d_out_p)).astype(bf16)
    return [*outs[:4], full, other, swap_core(att), in_columns(grad)]


def in_columns(g):
    rows, cols = g.shape
    return g.reshape(rows, PIECES, cols // PIECES).transpose(1, 0, 2)


def feed_kernel(comm, d_out, slope, b_own, b_oth, i_own, i_oth, resid, dout_rows, norms, o_own, o_oth, a_two, g_back, *refs):
    (grad, d_resid, low, d_att, two_norm, sent, part_back, stage, theirs, lhs, dz, wo, lows, lsem, send, recv) = refs[:16]
    step = pl.program_id(0)
    nb = theirs.shape[0]
    tm, d = resid.shape
    pro = dz.shape[0] // tm
    half = d // 2
    np_ = d // 128
    core = lax.axis_index("core")
    lo = pl.multiple_of(core * half, half)
    hi = pl.multiple_of((1 - core) * half, half)
    loads = [
        pltpu.make_async_copy(a_two, lhs.at[0], lsem.at[0]),
        pltpu.make_async_copy(o_own, wo.at[:, pl.ds(lo, half)], lsem.at[1]),
        pltpu.make_async_copy(o_oth, wo.at[:, pl.ds(hi, half)], lsem.at[2]),
    ]

    def hand(j):
        return hand_over(stage.at[j], theirs.at[j], send.at[1 + j], recv.at[1 + j])

    def hand_low(r):
        at = pl.ds(pl.multiple_of(r * tm, tm), tm)
        return hand_over(lows.at[at, :], sent.at[at, :], send.at[1 + nb + r], recv.at[1 + nb + r])

    @pl.when(step == 0)
    def _():
        for cp in loads:
            cp.start()

    if comm:
        swap = hand_over(a_two, lhs.at[1], send.at[0], recv.at[0])
        held, far, near, mid, total, keep = refs[16:22]
        scat = Scatter(g_back, held, far, near, mid, total, send, recv, 1 + nb + pro, part_back, keep)
        acts = (scat.begin, scat.turn, scat.close)

        @pl.when(step == 0)
        def _():
            load = pltpu.make_async_copy(g_back, held, lsem.at[3])
            load.start()
            greet([peer("core"), peer("x"), peer("y")])
            run_plan(acts, FEED_PLAN[0])
            swap.start()
            load.wait()

        for at, codes in enumerate(FEED_PLAN[:-1]):
            if codes and at > 0:
                pl.when(step == at)(functools.partial(run_plan, acts, codes))

        @pl.when((step > 0) & (step <= nb))
        def _():
            hand(step - 1).start()

    @pl.when(step < 2 * nb)
    def _():
        first = step < nb
        g = (dot_nt(d_out[...], pick(first, b_oth[...], b_own[...])) * slope[...].astype(f32)).astype(bf16)
        stage[step] = g
        more = dot_nt(g, pick(first, i_oth[...], i_own[...]))

        @pl.when(step == 0)
        def _():
            dz[...] = more

        @pl.when(step > 0)
        def _():
            dz[...] += more

    @pl.when(step == 2 * nb)
    def _():
        loads[0].wait()
        if comm:
            swap.wait()

    if comm:
        for j in range(nb):

            @pl.when(step == 2 * nb + j)
            def _():
                hand(j).wait()

    @pl.when((step >= 2 * nb) & (step < 3 * nb))
    def _():
        j = step - 2 * nb
        g = dot_tn(lhs[0], stage[nb + j])
        if comm:
            g = g + dot_tn(lhs[1], theirs[j])
        store_columns(grad, g)

    @pl.when(step == 3 * nb)
    def _():
        loads[1].wait()
        loads[2].wait()
        two_norm[...] = jnp.zeros_like(two_norm)

    @pl.when(step >= 3 * nb)
    def _():
        here = pl.ds(pl.multiple_of((step - 3 * nb) * tm, tm), tm)
        dv, g, b = layer_norm_back(resid[...], gain_row(norms, 2, d), dz[here, :])
        two_norm[0:np_, :] += flat_row(g)
        two_norm[np_:, :] += flat_row(b)
        dr = dout_rows[...].astype(f32) + dv
        d_resid[...] = dr
        dl = dr.astype(bf16)
        low[...] = dl
        lows[here, :] = pick(core == 0, dl[:, half:], dl[:, :half])
        d_att[:, :half] = dot_nt(dl, wo[pl.ds(lo, half), :]).astype(bf16)
        d_att[:, half:] = dot_nt(dl, wo[pl.ds(hi, half), :]).astype(bf16)
        if comm:
            hand_low(step - 3 * nb).start()

    if comm:

        @pl.when(step == pl.num_programs(0) - 1)
        def _():
            run_plan(acts, FEED_PLAN[-1])
            scat.finish()
            for r in range(pro):
                hand_low(r).wait()


def feed_back(d_out, slope, b_own, b_oth, i_own, i_oth, resid, norms, o_own, o_oth, a_two, g_back, n, comm, tm=256, blk=512):
    t, d = d_out.shape
    half = b_own.shape[0]
    nb = half // blk
    pro = t // tm
    oth = lambda i: jnp.minimum(i, nb - 1)
    own = lambda i: jnp.clip(i - nb, 0, nb - 1)
    row = lambda i: jnp.clip(i - 3 * nb, 0, pro - 1)
    rows = lambda w: pl.BlockSpec((tm, w), lambda i: (row(i), 0))
    whole = lambda s: pl.BlockSpec(s, lambda i: (0, 0))
    pieces, g_rows, g_cols = g_back.shape
    part = (pieces, g_rows // n, g_cols)
    per = half // PIECES
    extra = scatter_scratch(*g_back.shape) + [pltpu.VMEM(part, bf16), dma(pieces)] if comm else []
    sems = 1 + nb + pro + 6 * pieces
    outs = pl.pallas_call(
        functools.partial(feed_kernel, comm),
        grid=(3 * nb + pro,),
        out_shape=[sds((PIECES, d, per), bf16), sds((t, d), f32), sds((t, d), bf16), sds((t, d), bf16), sds((d // 64, 128), f32),
                   sds((t, d // 2), bf16), sds(part, bf16)],
        in_specs=[whole((t, d)), pl.BlockSpec((t, blk), lambda i: (0, jnp.where(i < nb, nb + i, own(i)))),
                  pl.BlockSpec((blk, d), lambda i: (own(i), 0)), pl.BlockSpec((blk, d), lambda i: (oth(i), 0)),
                  pl.BlockSpec((d, blk), lambda i: (0, own(i))), pl.BlockSpec((d, blk), lambda i: (0, oth(i))),
                  rows(d), rows(d), whole(norms.shape), ANY, ANY, ANY, ANY],
        out_specs=[pl.BlockSpec((blk // per, d, per), lambda i: (jnp.clip(i - 2 * nb, 0, nb - 1), 0, 0)), rows(d), rows(d), rows(d),
                   whole((d // 64, 128)), ANY, ANY],
        scratch_shapes=[pltpu.VMEM((2 * nb, t, blk), bf16), pltpu.VMEM((nb, t, blk), bf16), pltpu.VMEM((2, t, d), bf16),
                        pltpu.VMEM((t, d), f32), pltpu.VMEM((d, d), bf16), pltpu.VMEM((t, d // 2), bf16), dma(4), dma(sems), dma(sems)]
        + extra,
        compiler_params=comm_params(4 if comm else None, 62),
        cost_estimate=cost(12 * t * d * half + 2 * t * d * d, 60e6),
        name="feed_back",
    )(d_out, slope, b_own, b_oth, i_own, i_oth, resid, d_out, norms, o_own, o_oth, a_two, g_back)
    if comm:
        return outs
    core = lax.axis_index("core")
    other = lax.dynamic_slice_in_dim(outs[2], (1 - core) * (d // 2), d // 2, 1)
    d_pre = pre_values(d_out, slope, b_own, b_oth)
    g_in = dot_tn(a_two, d_pre[:, :half]) + dot_tn(swap_core(a_two), swap_core(d_pre[:, half:]))
    return [in_columns(g_in.astype(bf16)), *outs[1:5], swap_core(other), scatter_pieces(g_back)]


def pre_values(d_out, slope, own, oth):
    both = jnp.concatenate([dot_nt(d_out, own), dot_nt(d_out, oth)], axis=1)
    return (both * slope.astype(f32)).astype(bf16)


def scatter_pieces(g):
    return lax.psum_scatter(g, ("y", "x"), scatter_dimension=1, tiled=True)


def last_kernel(cfg, g1, g2, g3, theirs, low, low_p, dq, dk, dv, tok, d_resid, norms, h_own, h_oth, resid, doc, two_norm,
                a_one, a_one_p, att, att_p, w_own, w_oth, b_own, b_oth, part_in, *refs):
    d, comm = cfg
    out, mixed, red_in, red_in_p, red_at, red_at_p, sums, w, wb, parts, held, lsem = refs[:12]
    step = pl.program_id(0)
    last = pl.num_programs(0) - 1
    np_ = held.shape[0]
    pro = (last - np_) // 2
    half = 3 * d // 2
    q = d // 2
    hb = b_own.shape[0]
    nb = d // 128
    core = lax.axis_index("core")
    early = [pltpu.make_async_copy(a, wb.at[pl.ds(i * d, d), :], lsem.at[i]) for i, a in enumerate((a_one, a_one_p, att, att_p))]
    mids = [
        pltpu.make_async_copy(w_own, w.at[:, pl.ds(0, half)], lsem.at[4]),
        pltpu.make_async_copy(w_oth, w.at[:, pl.ds(half, half)], lsem.at[5]),
    ]
    late = [
        pltpu.make_async_copy(b_own, wb.at[pl.ds(0, hb), :], lsem.at[6]),
        pltpu.make_async_copy(b_oth, wb.at[pl.ds(hb, hb), :], lsem.at[7]),
    ]
    if comm:
        send, recv, mine_in, fi, sc, fa, vec, box, k_in, k_at = (
            refs[12], refs[13], refs[14], refs[15:19], refs[19:22], refs[22:27], refs[27], refs[28], refs[29], refs[30]
        )
        fold_in = Fold(
            pieces_of(part_in), pieces_of(mine_in), *fi, red_in, red_in_p, k_in, send, recv, 0
        )
        scat = Scatter(held, held, *sc, fa[0], send, recv, 4 * PIECES)
        mine_at = pieces_of(fa[0])
        fold_at = Fold(mine_at, mine_at, *fa[1:5], red_at, red_at_p, k_at, send, recv, 4 * PIECES + 6 * np_)
        base = 4 * PIECES + 10 * np_

        def note(i, src, dst, to):
            return pltpu.make_async_remote_copy(
                src_ref=src, dst_ref=dst, send_sem=send.at[base + i], recv_sem=recv.at[base + i], device_id=to, device_id_type=MESH
            )

        near, far = Fold.peers()
        notes = [
            note(0, vec.at[0], box.at[0], peer("x")),
            note(1, vec.at[1], box.at[1], peer("y")),
            note(2, vec.at[2], box.at[2], peer("core")),
            note(3, vec.at[3], box.at[3], near),
            note(4, vec.at[4], box.at[4], far),
            note(5, vec.at[5], vec.at[5], near),
        ]

        def norm_sum(k):
            if k < 3:
                notes[k].wait_recv()
                vec[k + 1] = vec[k] + box[k]
                if k < 2:
                    notes[k + 1].start()
                else:
                    pl.when(fold_in.end)(notes[3].start)
            elif k < 5:

                @pl.when(fold_in.mid)
                def _():
                    notes[k].wait_recv()
                    vec[k + 1] = vec[k] + box[k]
                    notes[k + 1].start()

            else:
                pl.when(fold_in.end)(notes[5].wait_recv)

        def settle(s):
            scat.close(s)
            fold_at.begin(s)

        acts = (scat.begin, scat.turn, settle, fold_in.inner, fold_in.outer, fold_in.land, fold_at.inner, fold_at.outer,
                fold_at.land, norm_sum)

    @pl.when(step == 0)
    def _():
        for cp in early + mids:
            cp.start()
        if comm:
            load = pltpu.make_async_copy(part_in, mine_in, lsem.at[8])
            load.start()
            greet([peer("core"), peer("x"), peer("y")] + Fold.peers())
            for s in range(PIECES):
                fold_in.begin(s)
            load.wait()
        for cp in early:
            cp.wait()
        parts[0 : 2 * nb, :] = jnp.zeros((2 * nb, 128), f32)
        parts[2 * nb :, :] = two_norm[...]

    if comm:
        for k, codes in enumerate(LAST_PLAN[:-1]):
            if codes:
                pl.when(step == k)(functools.partial(run_plan, acts, codes))

    per = q // g1.shape[1]

    @pl.when(step < 3 * per)
    def _():
        g = pick(step < per, g1[...], pick(step < 2 * per, g2[...], g3[...]))
        acc = dot_tn(wb[0:d, :], g) + dot_tn(wb[d : 2 * d, :], theirs[...])
        held[step] = acc.astype(bf16)

    @pl.when((step >= 3 * per) & (step < np_))
    def _():
        lo = pl.ds(pl.multiple_of(core * q, q), q)
        hi = pl.ds(pl.multiple_of((1 - core) * q, q), q)
        own = dot_tn(wb[2 * d : 3 * d, :q], low[...]) + dot_tn(wb[3 * d :, q:], low_p[...])
        held[step, lo, :] = own.astype(bf16)
        other = dot_tn(wb[2 * d : 3 * d, q:], low[...]) + dot_tn(wb[3 * d :, :q], low_p[...])
        held[step, hi, :] = other.astype(bf16)

    @pl.when(step == np_)
    def _():
        for cp in late:
            cp.start()
        for cp in mids:
            cp.wait()

    @pl.when((step >= np_) & (step < np_ + pro))
    def _():
        both = jnp.concatenate([g[:, :q] for g in (dq, dk, dv)] + [g[:, q:] for g in (dq, dk, dv)], axis=1)
        dz = dot_nt(both, w[...])
        grad, g, b = layer_norm_back(tok[...].astype(f32), gain_row(norms, 0, d), dz)
        parts[0:nb, :] += flat_row(g)
        parts[nb : 2 * nb, :] += flat_row(b)
        out[...] = (d_resid[...] + grad).astype(bf16)

    @pl.when(step == np_ + pro)
    def _():
        for cp in late:
            cp.wait()
        if comm:
            vec[0] = parts[...]
            notes[0].start()

    @pl.when((step >= np_ + pro) & (step < last))
    def _():
        y = dot_nn(h_own[...], wb[:hb, :]) + dot_nn(h_oth[...], wb[hb:, :]) + resid[...]
        mixed[...] = jnp.where(doc[...] >= 0, y, 0.0).astype(bf16)

    @pl.when(step == last)
    def _():
        if comm:
            run_plan(acts, LAST_PLAN[-1])
            fold_in.finish()
            scat.finish()
            fold_at.finish()
            for i in (0, 1, 2):
                notes[i].wait_send()
            pl.when(fold_in.end)(notes[3].wait_send)

            @pl.when(fold_in.mid)
            def _():
                notes[4].wait_send()
                notes[5].wait_send()

            sums[...] = vec[5]
        else:
            sums[...] = parts[...]
            cp = pltpu.make_async_copy(held, red_at, lsem.at[0])
            cp.start()
            cp.wait()


def flat_row(v):
    return jnp.concatenate([v[:, i * 128 : (i + 1) * 128] for i in range(v.shape[1] // 128)], axis=0)


def last_grad(grads3, theirs, low, low_p, tok, d_resid, norms, hidden, resid, doc_col, two_norm, a_one, a_one_p, att, att_p,
              own, oth, b_own, b_oth, part_in, n, comm, tm=256, wide=256):
    t, d = tok.shape
    pro = t // tm
    half = b_own.shape[0]
    q = d // 2
    per = q // wide
    np_ = 4 * per
    one = lambda w, c=0: pl.BlockSpec((tm, w), lambda i: (jnp.clip(i - np_, 0, pro - 1), c))
    two = lambda w, c=0: pl.BlockSpec((tm, w), lambda i: (jnp.clip(i - np_ - pro, 0, pro - 1), c))
    whole = lambda a: pl.BlockSpec(a.shape, lambda i: (0, 0))
    col = lambda k, count: pl.BlockSpec((t, wide), lambda i: (0, jnp.clip(i - k * per, 0, count - 1)))
    low_col = pl.BlockSpec((t, wide), lambda i: (0, lax.axis_index("core") * per + jnp.clip(i - 3 * per, 0, per - 1)))
    nv = 4 * d // 128
    pieced = part_in.shape
    share = (np_, d // n if comm else d, wide)
    slots = 4 * PIECES + 10 * np_ + 6
    extra = []
    if comm:
        extra = [dma(slots), dma(slots), pltpu.VMEM(part_in.shape, bf16)] + fold_scratch(*part_in.shape)
        extra += scatter_scratch(np_, d, wide)[1:] + [pltpu.VMEM(share, bf16)] * 5
        extra += [pltpu.VMEM((6, nv, 128), f32), pltpu.VMEM((5, nv, 128), f32), dma(PIECES), dma(np_)]
    return pl.pallas_call(
        functools.partial(last_kernel, (d, comm)),
        grid=(np_ + 2 * pro + 1,),
        out_shape=[sds((t, d), bf16), sds((t, d), bf16)] + [sds(pieced, bf16)] * 2 + [sds(share, bf16)] * 2 + [sds((nv, 128), f32)],
        in_specs=[col(0, per), col(1, per), col(2, per), col(0, 3 * per), low_col, col(3, per)]
        + [one(d)] * 5 + [whole(norms), two(half), two(half, 1), two(d), two(1), whole(two_norm)] + [ANY] * 9,
        out_specs=[one(d), two(d), ANY, ANY, ANY, ANY, pl.BlockSpec((nv, 128), lambda i: (0, 0))],
        scratch_shapes=[pltpu.VMEM((d, 3 * d), bf16), pltpu.VMEM((4 * d, d), bf16), pltpu.VMEM((nv, 128), f32),
                        pltpu.VMEM((np_, d, wide), bf16), dma(9)] + extra,
        compiler_params=comm_params(7 if comm else None, 63),
        cost_estimate=cost(14 * t * d * d + 4 * t * d * half, 60e6),
        name="last_grad",
    )(*grads3, theirs, low, low_p, *grads3, tok, d_resid, norms, hidden, hidden, resid, doc_col, two_norm,
      a_one, a_one_p, att, att_p, own, oth, b_own, b_oth, part_in)


def adam_update(g_ref, m1, m2, wg, st, mn):
    rows = g_ref.shape[0]
    step = min(rows, 256)

    @pl.loop(0, rows // step)
    def _(i):
        at = pl.ds(pl.multiple_of(i * step, 8), step)
        g = g_ref[at, :]
        first = BETA_ONE * m1[at, :] + (1.0 - BETA_ONE) * g
        second_hat = (BETA_TWO / (1.0 - BETA_TWO**STEPS)) * m2[at, :] + ((1.0 - BETA_TWO) / (1.0 - BETA_TWO**STEPS)) * g * g
        wg[at, :] = g
        st[at, :] = (-RATE / (1.0 - BETA_ONE**STEPS)) * first / (second_hat * lax.rsqrt(second_hat) + ADAM_EPS)
        mn[at, :] = first


def adam_kernel(plan, inv_root, own, oth, m1, m2, *refs):
    wg, st, mn, flat = refs[-4:]
    rows, stride, places = plan
    first = lax.axis_index("core") == 0
    wide = own.shape[2]
    for col, lo, hi in places:
        p, c = col // wide, col % wide
        a = own[p, :, c : c + 128].astype(f32) * inv_root
        b = oth[p, :, c : c + 128].astype(f32) * inv_root
        flat[pl.ds(lo, rows, stride=stride), :] = pick(first, a, b)
        flat[pl.ds(hi, rows, stride=stride), :] = pick(first, b, a)
    adam_update(flat, m1, m2, wg, st, mn)


def adam_columns(own, oth, at, count, m1, m2, prev, inv_root, first_row, rows, places):
    total, wide = own.shape[1:]
    nb = 2 * count * wide // 128
    blk = rows * nb
    assert first_row % blk == 0
    base = first_row // blk
    half = pl.BlockSpec((count, rows, wide), lambda i: (at, i, 0))
    flat = pl.BlockSpec((blk, 128), lambda i: (base + i, 0))
    kernel = functools.partial(adam_kernel, (rows, nb, places), inv_root)
    return adam_call(kernel, (total // rows,), own, oth, m1, m2, prev, half, flat, blk, "adam")


def adam_call(kernel, grid, own, oth, m1, m2, prev, half, flat, blk, name):
    return pl.pallas_call(
        kernel,
        grid=grid,
        out_shape=[sds(m1.shape, f32)] * 3,
        in_specs=[half, half, flat, flat] + [ANY] * len(prev),
        out_specs=[flat] * 3,
        scratch_shapes=[pltpu.VMEM((blk, 128), f32)],
        input_output_aliases={4 + i: i for i in range(len(prev))},
        compiler_params=params(),
        cost_estimate=cost(0, own.size * 2 * 22),
        name=name,
    )(own, oth, m1, m2, *prev)


def adam_rows_kernel(inv_root, own, oth, m1, m2, *refs):
    wg, st, mn, flat = refs[-4:]
    g = pick(pl.program_id(0) == lax.axis_index("core"), own[...], oth[...]).astype(f32) * inv_root
    rows, width = g.shape
    nb = width // 128
    for w in range(nb):
        flat[pl.ds(w, rows, stride=nb), :] = g[:, w * 128 : (w + 1) * 128]
    adam_update(flat, m1, m2, wg, st, mn)


def adam_rows_halves(own, oth, m1, m2, prev, inv_root, first_row):
    count, width = own.shape
    rows = count // 4
    blk = rows * width // 128
    base = first_row // blk
    half = pl.BlockSpec((rows, width), lambda h, i: (i, 0))
    flat = pl.BlockSpec((blk, 128), lambda h, i: (base + h * 4 + i, 0))
    kernel = functools.partial(adam_rows_kernel, inv_root)
    return adam_call(kernel, (2, 4), own, oth, m1, m2, prev, half, flat, blk, "adam_rows")


def adam_tail_kernel(g, m1, m2, p1, p2, p3, wg, st, mn):
    adam_update(g, m1, m2, wg, st, mn)


def adam_tail(g, m1, m2, prev, first_row):
    rows = 8
    assert first_row % rows == 0 and g.shape[0] <= rows
    g = jnp.pad(g, ((0, rows - g.shape[0]), (0, 0)))
    flat = pl.BlockSpec((rows, 128), lambda i: (first_row // rows, 0))
    return pl.pallas_call(
        adam_tail_kernel,
        grid=(1,),
        out_shape=[sds(m1.shape, f32)] * 3,
        in_specs=[pl.BlockSpec((rows, 128), lambda i: (0, 0)), flat, flat] + [ANY] * 3,
        out_specs=[flat] * 3,
        input_output_aliases={3: 0, 4: 1, 5: 2},
        name="adam_norms",
    )(g, m1, m2, *prev)


BLOCK = 4096


def adam_all_kernel(cfg, b_own, b_oth, i_own, i_oth, a_own, a_oth, norm, m1, m2, wg, st, mn, flat, later):
    inv_root, at_in, at_at, counts = cfg
    step = pl.program_id(0)
    core = lax.axis_index("core")
    first = core == 0
    n_back, n_in, n_at = counts

    @pl.when(step < n_back)
    def _():
        mine = step // (n_back // 2) == core
        pieces, rows, wide = b_own.shape
        for w in range(pieces * wide // 128):
            p, c = w * 128 // wide, w * 128 % wide
            g = pick(mine, b_own[p, :, c : c + 128], b_oth[p, :, c : c + 128])
            flat[pl.ds(w, rows, stride=pieces * wide // 128), :] = g.astype(f32) * inv_root

    def spread_columns(dst, own, oth, places):
        rows, wide = own.shape[1:]
        for col, lo, hi, stride in places:
            p, c = col // wide, col % wide
            a = own[p, :, c : c + 128].astype(f32) * inv_root
            b = oth[p, :, c : c + 128].astype(f32) * inv_root
            dst[pl.ds(lo, rows, stride=stride), :] = pick(first, a, b)
            dst[pl.ds(hi, rows, stride=stride), :] = pick(first, b, a)

    @pl.when((step >= n_back) & (step < n_back + n_in))
    def _():
        spread_columns(flat, i_own, i_oth, at_in)

    for k, places in enumerate(at_at):
        pl.when(step == k)(functools.partial(spread_columns, later, a_own, a_oth, places))

    @pl.when((step >= n_back + n_in) & (step < n_back + n_in + n_at))
    def _():
        at = pl.multiple_of((step - n_back - n_in) * BLOCK, BLOCK)
        flat[...] = later[pl.ds(at, BLOCK), :]

    @pl.when(step == n_back + n_in + n_at)
    def _():
        per = norm.shape[0] // 4
        at = pl.multiple_of(lax.axis_index(("y", "x")) * per, per)
        flat[0:per, :] = norm[pl.ds(at, per), :] * inv_root

    adam_update(flat, m1, m2, wg, st, mn)


def adam_all(back, inner, attention, norm, m1, m2, inv_root, places):
    at_in, at_qkv, at_out = places
    b_np, b_rows, b_wide = back[0].shape
    i_np, i_rows, i_wide = inner[0].shape
    np_, a_rows, wide = attention[0].shape
    n_back = 2 * b_np * b_rows * b_wide // 128 // BLOCK
    n_in = 2 * i_np * i_rows * i_wide // 128 // BLOCK
    n_at = 2 * np_ * a_rows * wide // 128 // BLOCK
    lots = np_ // (n_back + n_in)
    assert np_ == lots * (n_back + n_in) and m1.shape[0] == (n_back + n_in + n_at) * BLOCK + 8
    s_in, s_qkv, s_out = 2 * i_np * i_wide // 128, 2 * len(at_qkv), 2 * len(at_out)
    edge = a_rows * s_qkv
    at_at = [[] for _ in range(n_back + n_in)]
    for col, lo, hi in at_qkv:
        at_at[col // wide // lots].append((col % (wide * lots), lo, hi, s_qkv))
    for col, lo, hi in at_out:
        col += len(at_qkv) * 128
        at_at[col // wide // lots].append((col % (wide * lots), edge + lo, edge + hi, s_out))
    cfg = (inv_root, [(c, lo, hi, s_in) for c, lo, hi in at_in], at_at, (n_back, n_in, n_at))
    after_at, after_in = n_at, n_at + n_in

    def where(i):
        back_or_in = jnp.where(i < n_back, after_in + i, after_at + i - n_back)
        return jnp.where(i < n_back + n_in, back_or_in, jnp.where(i < n_back + n_in + n_at, i - n_back - n_in, i))

    flat = pl.BlockSpec((BLOCK, 128), lambda i: (where(i), 0))
    b_spec = pl.BlockSpec((b_np, 2 * b_rows // n_back, b_wide), lambda i: (0, jnp.minimum(i, n_back - 1) % (n_back // 2), 0))
    i_spec = pl.BlockSpec((i_np, i_rows // n_in, i_wide), lambda i: (0, jnp.clip(i - n_back, 0, n_in - 1), 0))
    a_spec = pl.BlockSpec((lots, a_rows, wide), lambda i: (jnp.minimum(i, n_back + n_in - 1), 0, 0))
    return pl.pallas_call(
        functools.partial(adam_all_kernel, cfg),
        grid=(n_back + n_in + n_at + 1,),
        out_shape=[sds(m1.shape, f32)] * 3,
        in_specs=[b_spec, b_spec, i_spec, i_spec, a_spec, a_spec, pl.BlockSpec(norm.shape, lambda i: (0, 0)), flat, flat],
        out_specs=[flat] * 3,
        scratch_shapes=[pltpu.VMEM((BLOCK, 128), f32), pltpu.VMEM((n_at * BLOCK, 128), f32)],
        compiler_params=params(),
        cost_estimate=cost(0, m1.size * 22),
        name="adam_all",
    )(*back, *inner, *attention, norm, m1, m2)


def after(x, *deps):
    return lax.optimization_barrier((x, deps))[0]


def body(n, nz, tokens, cotangent, doc_ids, master, moment_one, moment_two):
    t, d = tokens.shape
    ff = (master.shape[0] * n - 4 * d) // (2 * d) - 2 * d
    me = lax.axis_index(("y", "x"))
    rows = d // n
    comm = n == 4 and nz == 4

    lanes = master.reshape(-1, 128)
    w, o, norm_share = unpack_first(lanes, n, d, ff)
    doc_row = doc_ids.reshape(1, t)
    doc_col = doc_ids.reshape(t, 1)
    d_out = jnp.where(doc_col >= 0, cotangent, jnp.zeros((), bf16))
    if not comm:
        w, o = spread(w), spread(o)
        norm_share = lax.all_gather(master[-(4 * d // n) :].astype(bf16), ("y", "x"), axis=0, tiled=True)
        norm_share = norm_share.astype(f32).reshape(-1, 128)
    a_one, qkv, in_own, bk_own, w_own, w_oth, o_own, o_oth, norms = project_qkv(lanes, tokens, norm_share, w, o, n, ff, comm)
    att, lse, in_own, in_oth, a_one_p, d_out_p = attend(qkv, doc_row, doc_col, in_own, a_one, d_out, d, comm)
    resid, a_two, hidden, slope, bk_own, bk_oth, att_p, g_back = middle(
        att, tokens, norms, o_own, o_oth, in_own, in_oth, bk_own, d_out, d_out_p, comm
    )
    g_in, d_resid, low, d_att, two_norm, low_p, part_back = feed_back(
        d_out, slope, bk_own, bk_oth, in_own, in_oth, resid, norms, o_own, o_oth, a_two, g_back, n, comm
    )
    dq, dk, dv, dqkv_p, red_back, part_in = attend_back(qkv, d_att, att, lse, doc_row, doc_col, part_back, g_in, d, n, comm)
    input_grad, mixed, red_in, red_in_p, red_at, red_at_p, sums = last_grad(
        [dq, dk, dv], dqkv_p, low, low_p, tokens, d_resid, norms, hidden, resid, doc_col, two_norm, a_one, a_one_p, att, att_p,
        w_own, w_oth, bk_own, bk_oth, part_in, n, comm,
    )
    red_in, red_at = (red_in, red_in_p), (red_at, red_at_p)
    if not comm:
        red_in, red_at = both_halves(part_in), both_halves(scatter_pieces(red_at[0]))
        sums = lax.psum(sums, ("z", "core", "y", "x"))

    inv_root = float(t * n * nz * 2) ** (-0.5)
    m1, m2 = moment_one.reshape(-1, 128), moment_two.reshape(-1, 128)
    nb = d // 128
    half = nb // 2
    hs = ff // n // 2
    r_qkv, r_out, r_in = rows * 3 * nb, rows * nb, rows * ff // 128
    back_at = r_qkv + r_out + r_in
    at_in = [(hs * j + q * 128, (2 * hs * j) // 128 + q, (2 * hs * j + hs) // 128 + q) for j in range(n) for q in range(hs // 128)]
    at_qkv = [((p * half + w) * 128, p * nb + w, p * nb + w + half) for p in range(3) for w in range(half)]
    at_out = [(w * 128, w, w + half) for w in range(half)]
    if comm:
        outs = adam_all(red_back, red_in, red_at, sums, m1, m2, inv_root, (at_in, at_qkv, at_out))
    else:
        plain = lambda v: v.transpose(1, 0, 2).reshape(v.shape[1], -1)
        count = red_at[0].shape[0]
        outs = adam_rows_halves(plain(red_back[0]), plain(red_back[1]), m1, m2, [], inv_root, back_at)
        outs = adam_columns(*red_in, 0, red_in[0].shape[0], m1, m2, outs, inv_root, r_qkv + r_out, rows // 8, at_in)
        outs = adam_columns(*red_at, 0, 3 * count // 4, m1, m2, outs, inv_root, 0, rows // 8, at_qkv)
        outs = adam_columns(*red_at, 3, count // 4, m1, m2, outs, inv_root, r_qkv, rows // 2, at_out)
        per = 4 * nb // n
        norm_part = lax.dynamic_slice_in_dim(sums, group_index(n) * per, per, 0) * inv_root
        outs = adam_tail(norm_part, m1, m2, outs, back_at + ff // n * nb)
    weight_grad, step, moment = [o.reshape(-1) for o in outs]
    return mixed, input_grad, weight_grad, step, moment


def solution(mesh):
    dp, n = mesh.shape["dp"], mesh.shape["group"]
    fine = Mesh(mesh.devices.reshape(dp // 2, 2, n // 2, 2), ("z", "core", "y", "x"))
    tok = ("z", "core", "y", "x")
    flat = P(("y", "x"))
    in_specs = (P(tok, None), P(tok, None), P(tok), flat, flat, flat)
    out_specs = (P(tok, None), P(tok, None), flat, flat, flat)
    return jax.shard_map(
        functools.partial(body, n, dp // 2), mesh=fine, in_specs=in_specs, out_specs=out_specs, check_vma=False
    )
```

profile of v0, /device:TPU:0, one launch (start us, length us, event | category | flops | bytes accessed | tf_op | source)
XLA Modules:
  0.0 363.3 jit_solution(12410738340906049281)
XLA Ops:
  0.6 0.7 broadcast_compare_fusion
  1.3 1.7 copy.15.doc_col.doc
  3.0 3.1 broadcast_select_fusion.d_out.dout_rows
  6.2 4.0 %unpack.1 = (bf16[1024,1536]{1,0:T(8,128)(2,1)}, bf16[1024,512]{1,0:T(8,128)(2,1)}, f32[8,128]{1,0:T(8,128)}) custom-call(f32[24584,128]{1,0:T(8,128)} %bitcast.8, f32[24584,128]{1,0:T(8,128)} %bitcast.9, f32[24584,128]{1,0:T(8,128)} %bitcast.10), custom_call_target="tpu_custom_call" | custom-call | tf_op jit(solution)/shard_map/unpack/pallas_call | solution.py:358
  10.2 46.2 %qkv.1 = (bf16[1024,1024]{1,0:T(8,128)(2,1)}, bf16[1024,3072]{1,0:T(8,128)(2,1)}, bf16[1024,2048]{1,0:T(8,128)(2,1)}, bf16[2048,1024]{1,0:T(8,128)(2,1)}, bf16[1...) custom-call(bf16[1024,1024]{1,0:T(8,128)(2,1)} %tok.5, ...), custom_call_target="tpu_custom_call", output_to_operand_aliasing={{4}: (4, {}), {6}: (6, {})} | custom-call | flops 6442450944 | bytes 40000000 | tf_op jit(solution)/shard_map/qkv/pallas_call | solution.py:535
  56.4 42.1 %attend.1 = (bf16[1024,1024]{1,0:T(8,128)(2,1)}, f32[8,2,1024]{2,1,0:T(2,128)}, bf16[1024,2048]{1,0:T(8,128)(2,1)}, bf16[1024,2048]{1,0:T(8,128)(2,1)}, bf16[102...) custom-call(bf16[1024,3072]{1,0:T(8,128)(2,1)} %get-tuple-element.58.q.k.v, ...), custom_call_target="tpu_custom_call", output_to_operand_aliasing={{2}: (5, {})} | custom-call | flops 8589934592 | bytes 10000000 | tf_op jit(solution)/shard_map/attend/pallas_call | solution.py:645
  98.5 44.3 %middle.1 = (f32[1024,1024]{1,0:T(8,128)}, bf16[1024,1024]{1,0:T(8,128)(2,1)}, bf16[1024,4096]{1,0:T(8,128)(2,1)}, bf16[1024,4096]{1,0:T(8,128)(2,1)}, bf16[2048...) custom-call(bf16[1024,1024]{1,0:T(8,128)(2,1)} %get-tuple-element.61, ...), custom_call_target="tpu_custom_call", output_to_operand_aliasing={{4}: (8, {})} | custom-call | flops 19327352832 | bytes 60000000 | tf_op jit(solution)/shard_map/middle/pallas_call | solution.py:978
  142.8 67.0 %feed_back.1 = (bf16[8,1024,256]{2,1,0:T(8,128)(2,1)}, f32[1024,1024]{1,0:T(8,128)}, bf16[1024,1024]{1,0:T(8,128)(2,1)}, bf16[1024,1024]{1,0:T(8,128)(2,1)}, f32...) custom-call(bf16[1024,1024]{1,0:T(8,128)(2,1)} %broadcast_select_fusion.d_out.dout_rows, ...), custom_call_target="tpu_custom_call" | custom-call | flops 27917287424 | bytes 60000000 | tf_op jit(solution)/shard_map/feed_back/pallas_call | solution.py:1142
  209.8 49.6 %attend_back.1 = (bf16[1024,1024]{1,0:T(8,128)(2,1)}, bf16[1024,1024]{1,0:T(8,128)(2,1)}, bf16[1024,1024]{1,0:T(8,128)(2,1)}, bf16[1024,1536]{1,0:T(8,128)(2,1)}...) custom-call(bf16[1024,3072]{1,0:T(8,128)(2,1)} %get-tuple-element.58.q.k.v, ...), custom_call_target="tpu_custom_call" | custom-call | flops 21474836480 | bytes 16000000 | tf_op jit(solution)/shard_map/attend_back/pallas_call | solution.py:836
  259.4 71.6 %last_grad.1 = (bf16[1024,1024]{1,0:T(8,128)(2,1)}, bf16[1024,1024]{1,0:T(8,128)(2,1)}, bf16[8,256,256]{2,1,0:T(8,128)(2,1)}, bf16[8,256,256]{2,1,0:T(8,128)(2,1...) custom-call(bf16[1024,1024]{1,0:T(8,128)(2,1)} %get-tuple-element.79.g1.dq, ...), custom_call_target="tpu_custom_call" | custom-call | flops 23622320128 | bytes 60000000 | tf_op jit(solution)/shard_map/last_grad/pallas_call | solution.py:1370
  331.0 0.0 copy-start.1
  331.0 28.2 %adam_all.1 = (f32[24584,128]{1,0:T(8,128)}, f32[24584,128]{1,0:T(8,128)}, f32[24584,128]{1,0:T(8,128)}) custom-call(bf16[8,512,128]{2,1,0:T(8,128)(2,1)} %get-tuple-element.95.b_own, bf16[8,512,128]{2,1,0:T(8,128)(2,1)} %get-tuple-element.96.b_oth, bf16[8,256,256]{2,1,0:T(8,128)(2,1)} %get-tuple-element.97.i_own, ...), custom_call_target="tpu_custom_call" | custom-call | bytes 69228544 | tf_op jit(solution)/shard_map/adam_all/pallas_call | solution.py:1561
  359.2 0.0 copy-start
  359.3 0.0 copy-done.1
  359.3 1.3 copy.24
  360.6 1.0 copy-done
  361.6 1.3 copy.25
Async XLA Ops:
  331.0 28.2 %copy-start.1 = (bf16[1024,1024]{1,0:T(8,128)(2,1)S(1)}, bf16[1024,1024]{1,0:T(8,128)(2,1)}, u32[]{:S(2)}) copy-start(bf16[1024,1024]{1,0:T(8,128)(2,1)} %get-tuple-element.110) | copy-start | bytes 6291460
  359.2 2.3 copy-start
where the time goes:
time: 368 us; the launch traced here: 363 us
  Pallas kernels  353 us (96%)
  local copies, waits for them, and re-layouts  5.36 us (1%)
  other arithmetic  3.82 us (1%)
    pallas_call x1, Pallas kernels, last_grad(): pl.pallas_call(functools.partial(last_kernel, (d, comm)), grid=(np_ + 2 *...  71.6 us
    pallas_call x1, Pallas kernels, feed_back(): pl.pallas_call(functools.partial(feed_kernel, comm), grid=(3 * nb + pro,)...  67 us
    pallas_call x1, Pallas kernels, attend_back(): pl.pallas_call(functools.partial(attend_back_kernel, (hd, comm)), grid=(p...  49.6 us
    pallas_call x1, Pallas kernels, project_qkv(): pl.pallas_call(functools.partial(qkv_kernel, (n, comm)), grid=(UNPACK_STE...  46.2 us
    pallas_call x1, Pallas kernels, middle(): pl.pallas_call(functools.partial(middle_kernel, (d, tm, blk, comm)), grid...  44.3 us
    pallas_call x1, Pallas kernels, attend(): pl.pallas_call(functools.partial(attend_kernel, (hd, comm)), grid=(pairs,...  42.1 us
    pallas_call x1, Pallas kernels, adam_all(): pl.pallas_call(functools.partial(adam_all_kernel, cfg), grid=(n_back + n_...  28.2 us

commit v1 on v0

--- a/solution.py
+++ b/solution.py
@@ -143,13 +143,7 @@
 
 
 def add_up(dst, a, b):
-    rows, cols = dst.shape
-    step = max(8, 16384 // cols)
-
-    @pl.loop(0, rows // step)
-    def _(i):
-        at = pl.ds(pl.multiple_of(i * step, 8), step)
-        dst[at, :] = (a[at, :].astype(f32) + b[at, :].astype(f32)).astype(bf16)
+    dst[...] = a[...] + b[...]
 
 
 class Fold:
@@ -377,9 +371,10 @@
 UNPACK_STEPS = 8
 
 
-def qkv_kernel(cfg, tok, norm_share, m_in, m_back, w_own_in, w_oth_in, o_own_in, o_oth_in, *refs):
+def qkv_kernel(cfg, tok, norm_share, m_in, m_back, w_own_in, w_oth_in, o_own_in, o_oth_in, cot, docs, *refs):
     n, comm = cfg
-    (a_out, qkv, own_in, own_bk, w_own, w_oth, o_own, o_oth, norms_out, norms, w, toks, acc, lsem, send, recv) = refs
+    (a_hbm, qkv_hbm, own_in, own_bk, w_own, w_oth, o_own, o_oth, norms_out, d_hbm, doc_col, norms, w, toks, acc, cots, qkv, a_out,
+     lsem, send, recv) = refs
     if not comm:
         w_own, w_oth = w_own_in, w_oth_in
     t, d = toks.shape
@@ -389,6 +384,9 @@
     share = d // n
     tm = min(256, t)
     tok_copy = pltpu.make_async_copy(tok, toks, lsem.at[0])
+    cot_copy = pltpu.make_async_copy(cot, cots, lsem.at[1 + 2 * n])
+    a_copy = pltpu.make_async_copy(a_out, a_hbm, lsem.at[2 + 2 * n])
+    d_copy = pltpu.make_async_copy(cots, d_hbm, lsem.at[3 + 2 * n])
 
     if comm:
         me = member()
@@ -410,6 +408,7 @@
     @pl.when(step == 0)
     def _():
         tok_copy.start()
+        cot_copy.start()
         if comm:
             greet(near + [peer("core")])
             for m in notes:
@@ -472,6 +471,15 @@
             a_out[at, :] = (xhat * gain + bias).astype(bf16)
 
         each_block(norm)
+        cot_copy.wait()
+        doc_col[...] = jnp.broadcast_to(docs[...].astype(f32), (128, t)).T[:, :1].astype(jnp.int32)
+
+        def mask(at):
+            cots[at, :] = jnp.where(doc_col[at, :] >= 0, cots[at, :].astype(f32), 0.0).astype(bf16)
+
+        each_block(mask)
+        a_copy.start()
+        d_copy.start()
         if comm:
             first.arrive(4)
         load(0)
@@ -510,13 +518,17 @@
                 qkv[at, o + q : o + half] = total[:, o + q : o + half].astype(bf16)
 
         each_block(last)
+        out = pltpu.make_async_copy(qkv, qkv_hbm, lsem.at[4 + 2 * n])
+        out.start()
         if comm:
             second.forward()
             second.finish()
             first.sent()
-
-
-def project_qkv(lanes, tok, norm_share, w, o, n, ff, comm):
+        for cp in (a_copy, d_copy, out):
+            cp.wait()
+
+
+def project_qkv(lanes, tok, cot, docs, norm_share, w, o, n, ff, comm):
     t, d = tok.shape
     rows = d // n
     nb = d // 128
@@ -530,7 +542,8 @@
     whole = lambda s: pl.BlockSpec(s, lambda i: (0, 0))
     half = 3 * d // 2
     shapes = [sds((t, d), bf16), sds((t, 3 * d), bf16), sds((d, ff // 2), bf16), sds((ff // 2, d), bf16),
-              sds((d, half), bf16), sds((d, half), bf16), sds((d, d // 2), bf16), sds((d, d // 2), bf16), sds((4 * nb, 128), f32)]
+              sds((d, half), bf16), sds((d, half), bf16), sds((d, d // 2), bf16), sds((d, d // 2), bf16), sds((4 * nb, 128), f32),
+              sds((t, d), bf16), sds((t, 1), jnp.int32)]
     w_args = [w, norm_share, o, norm_share] if comm else [w[0], w[1], o[0], o[1]]
     outs = pl.pallas_call(
         functools.partial(qkv_kernel, (n, comm)),
@@ -540,24 +553,25 @@
             ANY, whole(norm_share.shape),
             pl.BlockSpec((b_in, 128), lambda i: (at_in // b_in + up(i), 0)),
             pl.BlockSpec((b_bk, 128), lambda i: (at_bk // b_bk + lax.axis_index("core") * UNPACK_STEPS + up(i), 0)),
-            ANY, ANY, ANY, ANY,
+            ANY, ANY, ANY, ANY, ANY, whole((1, t)),
         ],
         out_specs=[
-            whole((t, d)), whole((t, 3 * d)),
+            ANY, ANY,
             pl.BlockSpec((rows // UNPACK_STEPS, ff // 2), lambda i: (me() * UNPACK_STEPS + up(i), 0)),
             pl.BlockSpec((hs // UNPACK_STEPS, d), lambda i: (me() * UNPACK_STEPS + up(i), 0)),
-            ANY, ANY, ANY, ANY, whole((4 * nb, 128)),
+            ANY, ANY, ANY, ANY, whole((4 * nb, 128)), ANY, whole((t, 1)),
         ],
         scratch_shapes=[pltpu.VMEM((4 * nb, 128), f32), pltpu.VMEM((n, rows, 3 * d), bf16), pltpu.VMEM((t, d), bf16),
-                        pltpu.VMEM((t, 3 * d), f32), dma(1 + 2 * n), dma(25), dma(25)],
+                        pltpu.VMEM((t, 3 * d), f32), pltpu.VMEM((t, d), bf16), pltpu.VMEM((t, 3 * d), bf16), pltpu.VMEM((t, d), bf16),
+                        dma(5 + 2 * n), dma(25), dma(25)],
         input_output_aliases={4: 4, 6: 6},
         compiler_params=comm_params(1 if comm else None),
         cost_estimate=cost(2 * t * d * 3 * d, 40e6),
         name="qkv",
-    )(tok, norm_share, lanes, lanes, *w_args)
+    )(tok, norm_share, lanes, lanes, *w_args, cot, docs)
     if comm:
         return outs
-    return [*outs[:4], w[0], w[1], o[0], o[1], outs[8]]
+    return [*outs[:4], w[0], w[1], o[0], o[1], *outs[8:]]
 
 
 QB = 256
@@ -1178,7 +1192,8 @@
 def last_kernel(cfg, g1, g2, g3, theirs, low, low_p, dq, dk, dv, tok, d_resid, norms, h_own, h_oth, resid, doc, two_norm,
                 a_one, a_one_p, att, att_p, w_own, w_oth, b_own, b_oth, part_in, *refs):
     d, comm = cfg
-    out, mixed, red_in, red_in_p, red_at, red_at_p, sums, w, wb, parts, held, lsem = refs[:12]
+    out, mixed, red_in, red_in_p, red_at, red_at_p, sums, w, wb, parts, held, lsem, total = refs[:13]
+    refs = refs[1:]
     step = pl.program_id(0)
     last = pl.num_programs(0) - 1
     np_ = held.shape[0]
@@ -1314,8 +1329,16 @@
 
     @pl.when((step >= np_ + pro) & (step < last))
     def _():
-        y = dot_nn(h_own[...], wb[:hb, :]) + dot_nn(h_oth[...], wb[hb:, :]) + resid[...]
-        mixed[...] = jnp.where(doc[...] >= 0, y, 0.0).astype(bf16)
+        total[...] = resid[...]
+        chunk = hb // 4
+
+        @pl.loop(0, 4)
+        def _(i):
+            at = pl.ds(pl.multiple_of(i * chunk, chunk), chunk)
+            beyond = pl.ds(pl.multiple_of(hb + i * chunk, chunk), chunk)
+            total[...] += dot_nn(h_own[:, at], wb[at, :]) + dot_nn(h_oth[:, at], wb[beyond, :])
+
+        mixed[...] = jnp.where(doc[...] >= 0, total[...], 0.0).astype(bf16)
 
     @pl.when(step == last)
     def _():
@@ -1375,7 +1398,7 @@
         + [one(d)] * 5 + [whole(norms), two(half), two(half, 1), two(d), two(1), whole(two_norm)] + [ANY] * 9,
         out_specs=[one(d), two(d), ANY, ANY, ANY, ANY, pl.BlockSpec((nv, 128), lambda i: (0, 0))],
         scratch_shapes=[pltpu.VMEM((d, 3 * d), bf16), pltpu.VMEM((4 * d, d), bf16), pltpu.VMEM((nv, 128), f32),
-                        pltpu.VMEM((np_, d, wide), bf16), dma(9)] + extra,
+                        pltpu.VMEM((np_, d, wide), bf16), dma(9), pltpu.VMEM((tm, d), f32)] + extra,
         compiler_params=comm_params(7 if comm else None, 63),
         cost_estimate=cost(14 * t * d * d + 4 * t * d * half, 60e6),
         name="last_grad",
@@ -1585,13 +1608,13 @@
     lanes = master.reshape(-1, 128)
     w, o, norm_share = unpack_first(lanes, n, d, ff)
     doc_row = doc_ids.reshape(1, t)
-    doc_col = doc_ids.reshape(t, 1)
-    d_out = jnp.where(doc_col >= 0, cotangent, jnp.zeros((), bf16))
     if not comm:
         w, o = spread(w), spread(o)
         norm_share = lax.all_gather(master[-(4 * d // n) :].astype(bf16), ("y", "x"), axis=0, tiled=True)
         norm_share = norm_share.astype(f32).reshape(-1, 128)
-    a_one, qkv, in_own, bk_own, w_own, w_oth, o_own, o_oth, norms = project_qkv(lanes, tokens, norm_share, w, o, n, ff, comm)
+    a_one, qkv, in_own, bk_own, w_own, w_oth, o_own, o_oth, norms, d_out, doc_col = project_qkv(
+        lanes, tokens, cotangent, doc_row, norm_share, w, o, n, ff, comm
+    )
     att, lse, in_own, in_oth, a_one_p, d_out_p = attend(qkv, doc_row, doc_col, in_own, a_one, d_out, d, comm)
     resid, a_two, hidden, slope, bk_own, bk_oth, att_p, g_back = middle(
         att, tokens, norms, o_own, o_oth, in_own, in_oth, bk_own, d_out, d_out_p, comm

time: 368 us -> 347 us (0.943); the launches traced: 363 us -> 346 us
  Pallas kernels: 353 us -> 342 us
  other arithmetic: 3.82 us -> 0 us
    pallas_call x1, Pallas kernels: 67 us -> 57.8 us  [feed_back(): pl.pallas_call(functools.partial(feed_kernel, comm), grid=(3 * nb + pro,)...]
where the time goes in v1:
time: 347 us; the launch traced here: 346 us
  Pallas kernels  342 us (99%)
  local copies, waits for them, and re-layouts  3.65 us (1%)
    pallas_call x1, Pallas kernels, last_grad(): pl.pallas_call(functools.partial(last_kernel, (d, comm)), grid=(np_ + 2 *...  72.4 us
    pallas_call x1, Pallas kernels, feed_back(): pl.pallas_call(functools.partial(feed_kernel, comm), grid=(3 * nb + pro,)...  57.8 us
    pallas_call x1, Pallas kernels, attend_back(): pl.pallas_call(functools.partial(attend_back_kernel, (hd, comm)), grid=(p...  49.6 us
    pallas_call x1, Pallas kernels, middle(): pl.pallas_call(functools.partial(middle_kernel, (d, tm, blk, comm)), grid...  44.5 us
    pallas_call x1, Pallas kernels, project_qkv(): pl.pallas_call(functools.partial(qkv_kernel, (n, comm)), grid=(UNPACK_STE...  44.1 us
    pallas_call x1, Pallas kernels, attend(): pl.pallas_call(functools.partial(attend_kernel, (hd, comm)), grid=(pairs,...  41.7 us
    pallas_call x1, Pallas kernels, adam_all(): pl.pallas_call(functools.partial(adam_all_kernel, cfg), grid=(n_back + n_...  27.9 us

profile of v1, /device:TPU:0, one launch (start us, length us, event | category | flops | bytes accessed | tf_op | source)
XLA Modules:
  0.0 346.4 jit_solution(16070577329762587126)
XLA Ops:
  0.6 4.1 %unpack.1 = (bf16[1024,1536]{1,0:T(8,128)(2,1)}, bf16[1024,512]{1,0:T(8,128)(2,1)}, f32[8,128]{1,0:T(8,128)}) custom-call(f32[24584,128]{1,0:T(8,128)} %bitcast.7, f32[24584,128]{1,0:T(8,128)} %bitcast.8, f32[24584,128]{1,0:T(8,128)} %bitcast.9), custom_call_target="tpu_custom_call" | custom-call | tf_op jit(solution)/shard_map/unpack/pallas_call | solution.py:352
  4.7 44.1 %qkv.1 = (bf16[1024,1024]{1,0:T(8,128)(2,1)}, bf16[1024,3072]{1,0:T(8,128)(2,1)}, bf16[1024,2048]{1,0:T(8,128)(2,1)}, bf16[2048,1024]{1,0:T(8,128)(2,1)}, bf16[1...) custom-call(bf16[1024,1024]{1,0:T(8,128)(2,1)} %tok.5, ...), custom_call_target="tpu_custom_call", output_to_operand_aliasing={{4}: (4, {}), {6}: (6, {})} | custom-call | flops 6442450944 | bytes 40000000 | tf_op jit(solution)/shard_map/qkv/pallas_call | solution.py:548
  48.8 41.7 %attend.1 = (bf16[1024,1024]{1,0:T(8,128)(2,1)}, f32[8,2,1024]{2,1,0:T(2,128)}, bf16[1024,2048]{1,0:T(8,128)(2,1)}, bf16[1024,2048]{1,0:T(8,128)(2,1)}, bf16[102...) custom-call(bf16[1024,3072]{1,0:T(8,128)(2,1)} %get-tuple-element.60.q.k.v, ...), custom_call_target="tpu_custom_call", output_to_operand_aliasing={{2}: (5, {})} | custom-call | flops 8589934592 | bytes 10000000 | tf_op jit(solution)/shard_map/attend/pallas_call | solution.py:659
  90.5 44.5 %middle.1 = (f32[1024,1024]{1,0:T(8,128)}, bf16[1024,1024]{1,0:T(8,128)(2,1)}, bf16[1024,4096]{1,0:T(8,128)(2,1)}, bf16[1024,4096]{1,0:T(8,128)(2,1)}, bf16[2048...) custom-call(bf16[1024,1024]{1,0:T(8,128)(2,1)} %get-tuple-element.65, ...), custom_call_target="tpu_custom_call", output_to_operand_aliasing={{4}: (8, {})} | custom-call | flops 19327352832 | bytes 60000000 | tf_op jit(solution)/shard_map/middle/pallas_call | solution.py:992
  135.1 57.8 %feed_back.1 = (bf16[8,1024,256]{2,1,0:T(8,128)(2,1)}, f32[1024,1024]{1,0:T(8,128)}, bf16[1024,1024]{1,0:T(8,128)(2,1)}, bf16[1024,1024]{1,0:T(8,128)(2,1)}, f32...) custom-call(bf16[1024,1024]{1,0:T(8,128)(2,1)} %get-tuple-element.61.d_out.dout_rows, ...), custom_call_target="tpu_custom_call" | custom-call | flops 27917287424 | bytes 60000000 | tf_op jit(solution)/shard_map/feed_back/pallas_call | solution.py:1156
  192.9 49.6 %attend_back.1 = (bf16[1024,1024]{1,0:T(8,128)(2,1)}, bf16[1024,1024]{1,0:T(8,128)(2,1)}, bf16[1024,1024]{1,0:T(8,128)(2,1)}, bf16[1024,1536]{1,0:T(8,128)(2,1)}...) custom-call(bf16[1024,3072]{1,0:T(8,128)(2,1)} %get-tuple-element.60.q.k.v, ...), custom_call_target="tpu_custom_call" | custom-call | flops 21474836480 | bytes 16000000 | tf_op jit(solution)/shard_map/attend_back/pallas_call | solution.py:850
  242.4 72.4 %last_grad.1 = (bf16[1024,1024]{1,0:T(8,128)(2,1)}, bf16[1024,1024]{1,0:T(8,128)(2,1)}, bf16[8,256,256]{2,1,0:T(8,128)(2,1)}, bf16[8,256,256]{2,1,0:T(8,128)(2,1...) custom-call(bf16[1024,1024]{1,0:T(8,128)(2,1)} %get-tuple-element.83.g1.dq, ...), custom_call_target="tpu_custom_call" | custom-call | flops 23622320128 | bytes 60000000 | tf_op jit(solution)/shard_map/last_grad/pallas_call | solution.py:1393
  314.8 0.0 copy-start.1
  314.8 27.9 %adam_all.1 = (f32[24584,128]{1,0:T(8,128)}, f32[24584,128]{1,0:T(8,128)}, f32[24584,128]{1,0:T(8,128)}) custom-call(bf16[8,512,128]{2,1,0:T(8,128)(2,1)} %get-tuple-element.99.b_own, bf16[8,512,128]{2,1,0:T(8,128)(2,1)} %get-tuple-element.100.b_oth, bf16[8,256,256]{2,1,0:T(8,128)(2,1)} %get-tuple-element.101.i_own, ...), custom_call_target="tpu_custom_call" | custom-call | bytes 69228544 | tf_op jit(solution)/shard_map/adam_all/pallas_call | solution.py:1584
  342.7 0.0 copy-start
  342.8 0.0 copy-done.1
  342.8 1.3 copy.21
  344.1 1.0 copy-done
  345.1 1.3 copy.22
Async XLA Ops:
  314.8 28.0 %copy-start.1 = (bf16[1024,1024]{1,0:T(8,128)(2,1)S(1)}, bf16[1024,1024]{1,0:T(8,128)(2,1)}, u32[]{:S(2)}) copy-start(bf16[1024,1024]{1,0:T(8,128)(2,1)} %get-tuple-element.114) | copy-start | bytes 6291460
  342.7 2.3 copy-start

commit v2 on v1

--- a/solution.py
+++ b/solution.py
@@ -58,11 +58,19 @@
     return {a: 1 - lax.axis_index(a) for a in axes}
 
 
-def greet(peers):
+def greet_start(peers):
     barrier = pltpu.get_barrier_semaphore()
     for p in peers:
         pl.semaphore_signal(barrier, inc=1, device_id=p, device_id_type=MESH)
-    pl.semaphore_wait(barrier, len(peers))
+
+
+def greet_end(peers):
+    pl.semaphore_wait(pltpu.get_barrier_semaphore(), len(peers))
+
+
+def greet(peers):
+    greet_start(peers)
+    greet_end(peers)
 
 
 def member():
@@ -72,7 +80,7 @@
 class Gather:
     COUNT = 11
 
-    def __init__(self, own, oth, send, recv, base):
+    def __init__(self, own, oth, send, recv, base, mine=None):
         rows = own.shape[0] // 4
         half = rows // 2
         x, y = lax.axis_index("x"), lax.axis_index("y")
@@ -81,8 +89,9 @@
 
         def move(i, k, off, count, dst, to):
             at = pl.ds(pl.multiple_of(share[k] * rows + off, 8), count)
+            here = own.at[at, :] if mine is None or k else mine.at[pl.ds(off, count), :]
             return pltpu.make_async_remote_copy(
-                src_ref=own.at[at, :], dst_ref=dst.at[at, :],
+                src_ref=here, dst_ref=dst.at[at, :],
                 send_sem=send.at[base + i], recv_sem=recv.at[base + i], device_id=peer(to), device_id_type=MESH,
             )
 
@@ -372,9 +381,9 @@
 
 
 def qkv_kernel(cfg, tok, norm_share, m_in, m_back, w_own_in, w_oth_in, o_own_in, o_oth_in, cot, docs, *refs):
-    n, comm = cfg
-    (a_hbm, qkv_hbm, own_in, own_bk, w_own, w_oth, o_own, o_oth, norms_out, d_hbm, doc_col, norms, w, toks, acc, cots, qkv, a_out,
-     lsem, send, recv) = refs
+    n, comm, hd = cfg
+    (a_hbm, qkv_hbm, in_own, own_bk, w_own, w_oth, o_own, o_oth, norms_out, d_hbm, doc_col, att, lse, in_oth, a_p, d_p,
+     norms, w, toks, acc, cots, qkv, a_out, own_in, bias, lsem, send, recv) = refs
     if not comm:
         w_own, w_oth = w_own_in, w_oth_in
     t, d = toks.shape
@@ -387,6 +396,9 @@
     cot_copy = pltpu.make_async_copy(cot, cots, lsem.at[1 + 2 * n])
     a_copy = pltpu.make_async_copy(a_out, a_hbm, lsem.at[2 + 2 * n])
     d_copy = pltpu.make_async_copy(cots, d_hbm, lsem.at[3 + 2 * n])
+    place = pl.ds(pl.multiple_of(group_index(n) * share, 8), share)
+    in_copy = pltpu.make_async_copy(own_in, in_own.at[place, :], lsem.at[5 + 2 * n])
+    out = pltpu.make_async_copy(qkv, qkv_hbm, lsem.at[4 + 2 * n])
 
     if comm:
         me = member()
@@ -401,6 +413,8 @@
         ]
         first = Gather(w_own, w_oth, send, recv, 0)
         second = Gather(o_own, o_oth, send, recv, 11)
+        third = Gather(in_own, in_oth, send, recv, 25, own_in)
+        swaps = [hand_over(a_out, a_p, send.at[36], recv.at[36]), hand_over(cots, d_p, send.at[37], recv.at[37])]
         rows = first.rows
     else:
         rows = [pl.ds(k * share, share) for k in range(n)]
@@ -419,14 +433,15 @@
     @pl.when(step < UNPACK_STEPS)
     def _():
         core = lax.axis_index("core")
-        rows_in = own_in.shape[0]
+        rows_in = own_in.shape[0] // UNPACK_STEPS
+        there = pl.ds(pl.multiple_of(step * rows_in, 8), rows_in)
         hs = own_in.shape[1] // n
         stride = m_in.shape[0] // rows_in
         for j in range(n):
             for q in range(hs // 128):
                 lo = (2 * hs * j) // 128 + q + core * (hs // 128)
                 at = hs * j + q * 128
-                own_in[:, at : at + 128] = m_in[pl.ds(lo, rows_in, stride=stride), :].astype(bf16)
+                own_in[there, at : at + 128] = m_in[pl.ds(lo, rows_in, stride=stride), :].astype(bf16)
         for q in range(nb):
             own_bk[:, q * 128 : (q + 1) * 128] = m_back[pl.ds(q, own_bk.shape[0], stride=nb), :].astype(bf16)
 
@@ -464,11 +479,11 @@
             norms[...] = norm_share[...]
         norms_out[...] = norms[...]
         tok_copy.wait()
-        gain, bias = gain_row(norms, 0, d), gain_row(norms, 1, d)
+        gain, shift = gain_row(norms, 0, d), gain_row(norms, 1, d)
 
         def norm(at):
             xhat, _ = layer_norm_parts(toks[at, :].astype(f32))
-            a_out[at, :] = (xhat * gain + bias).astype(bf16)
+            a_out[at, :] = (xhat * gain + shift).astype(bf16)
 
         each_block(norm)
         cot_copy.wait()
@@ -480,6 +495,8 @@
         each_block(mask)
         a_copy.start()
         d_copy.start()
+        in_copy.start()
+        fill_bias(bias, docs, doc_col)
         if comm:
             first.arrive(4)
         load(0)
@@ -493,6 +510,7 @@
     def _():
         if comm:
             first.forward()
+            third.begin()
             first.arrive(7, 8)
         load(*range(1, n - 1))
 
@@ -518,106 +536,51 @@
                 qkv[at, o + q : o + half] = total[:, o + q : o + half].astype(bf16)
 
         each_block(last)
-        out = pltpu.make_async_copy(qkv, qkv_hbm, lsem.at[4 + 2 * n])
         out.start()
+
+    start = UNPACK_STEPS + 3
+    if comm:
+
+        @pl.when(step == start + 1)
+        def _():
+            second.forward()
+            for m in swaps:
+                m.start()
+
+        @pl.when(step == start + 3)
+        def _():
+            third.relay()
+
+        @pl.when(step == start + 6)
+        def _():
+            third.forward()
+            second.close()
+
+    @pl.when(step >= start)
+    def _():
+        pair = step - start
+        pairs = d // 256
+        first_col = (pair // pairs) * half + (pair % pairs) * 128
+
+        def part(k):
+            return qkv.at[:, pl.ds(pl.multiple_of(first_col + k * (d // 2), 128), 128)]
+
+        attend_pair(hd, part(0), part(1), part(2), bias, att, lse)
+
+    @pl.when(step == pl.num_programs(0) - 1)
+    def _():
         if comm:
-            second.forward()
-            second.finish()
+            third.finish()
+            second.arrive(4, 7, 8, 9, 10)
+            second.sent()
             first.sent()
-        for cp in (a_copy, d_copy, out):
+            for m in swaps:
+                m.wait()
+        for cp in (a_copy, d_copy, in_copy, out):
             cp.wait()
 
 
-def project_qkv(lanes, tok, cot, docs, norm_share, w, o, n, ff, comm):
-    t, d = tok.shape
-    rows = d // n
-    nb = d // 128
-    hs = ff // n // 2
-    r_in, r_bk = rows * ff // 128, ff // n * nb
-    at_in, at_bk = rows * 4 * nb, rows * 4 * nb + r_in
-    b_in, b_bk = r_in // UNPACK_STEPS, hs * nb // UNPACK_STEPS
-    assert at_in % b_in == 0 and at_bk % b_bk == 0
-    up = lambda i: jnp.minimum(i, UNPACK_STEPS - 1)
-    me = lambda: group_index(n)
-    whole = lambda s: pl.BlockSpec(s, lambda i: (0, 0))
-    half = 3 * d // 2
-    shapes = [sds((t, d), bf16), sds((t, 3 * d), bf16), sds((d, ff // 2), bf16), sds((ff // 2, d), bf16),
-              sds((d, half), bf16), sds((d, half), bf16), sds((d, d // 2), bf16), sds((d, d // 2), bf16), sds((4 * nb, 128), f32),
-              sds((t, d), bf16), sds((t, 1), jnp.int32)]
-    w_args = [w, norm_share, o, norm_share] if comm else [w[0], w[1], o[0], o[1]]
-    outs = pl.pallas_call(
-        functools.partial(qkv_kernel, (n, comm)),
-        grid=(UNPACK_STEPS + 3,),
-        out_shape=shapes,
-        in_specs=[
-            ANY, whole(norm_share.shape),
-            pl.BlockSpec((b_in, 128), lambda i: (at_in // b_in + up(i), 0)),
-            pl.BlockSpec((b_bk, 128), lambda i: (at_bk // b_bk + lax.axis_index("core") * UNPACK_STEPS + up(i), 0)),
-            ANY, ANY, ANY, ANY, ANY, whole((1, t)),
-        ],
-        out_specs=[
-            ANY, ANY,
-            pl.BlockSpec((rows // UNPACK_STEPS, ff // 2), lambda i: (me() * UNPACK_STEPS + up(i), 0)),
-            pl.BlockSpec((hs // UNPACK_STEPS, d), lambda i: (me() * UNPACK_STEPS + up(i), 0)),
-            ANY, ANY, ANY, ANY, whole((4 * nb, 128)), ANY, whole((t, 1)),
-        ],
-        scratch_shapes=[pltpu.VMEM((4 * nb, 128), f32), pltpu.VMEM((n, rows, 3 * d), bf16), pltpu.VMEM((t, d), bf16),
-                        pltpu.VMEM((t, 3 * d), f32), pltpu.VMEM((t, d), bf16), pltpu.VMEM((t, 3 * d), bf16), pltpu.VMEM((t, d), bf16),
-                        dma(5 + 2 * n), dma(25), dma(25)],
-        input_output_aliases={4: 4, 6: 6},
-        compiler_params=comm_params(1 if comm else None),
-        cost_estimate=cost(2 * t * d * 3 * d, 40e6),
-        name="qkv",
-    )(tok, norm_share, lanes, lanes, *w_args, cot, docs)
-    if comm:
-        return outs
-    return [*outs[:4], w[0], w[1], o[0], o[1], *outs[8:]]
-
-
-QB = 256
-
-
-def fill_bias(bias, doc_row, doc_col):
-    t = bias.shape[0]
-    for r in range(0, t, QB):
-        key = r + lax.broadcasted_iota(jnp.int32, (QB, t), 0)
-        query = lax.broadcasted_iota(jnp.int32, (QB, t), 1)
-        ok = (doc_col[r : r + QB, :] == doc_row[...]) & (key <= query)
-        bias[r : r + QB, :] = jnp.where(ok, 0.0, FILL)
-
-
-def head_lanes(v, h, hd):
-    lane = lax.broadcasted_iota(jnp.int32, v.shape, 1)
-    return jnp.where((lane >= h * hd) & (lane < (h + 1) * hd), v, jnp.zeros_like(v))
-
-
-def attend_kernel(cfg, q, k, v, doc_row, doc_col, w_own_in, a_one, d_out, out, lse, w_own, w_oth, a_p, d_p, bias, send, recv):
-    hd, comm = cfg
-    step = pl.program_id(0)
-    last = pl.num_programs(0) - 1
-    if comm:
-        gather = Gather(w_own, w_oth, send, recv, 0)
-        swaps = [hand_over(a_one, a_p, send.at[11], recv.at[11]), hand_over(d_out, d_p, send.at[12], recv.at[12])]
-
-        @pl.when(step == 0)
-        def _():
-            greet([peer("x"), peer("y"), peer("core")])
-            gather.begin()
-            for s in swaps:
-                s.start()
-
-        @pl.when(step == 4)
-        def _():
-            gather.relay()
-
-        @pl.when(step == 6)
-        def _():
-            gather.forward()
-
-    @pl.when(step == 0)
-    def _():
-        fill_bias(bias, doc_row, doc_col)
-
+def attend_pair(hd, q, k, v, bias, out, lse):
     t = q.shape[0]
     vt = v[...].T
     per = 128 // hd
@@ -636,44 +599,78 @@
             outs.append(o * (1.0 / total))
         out[cols, :] = jnp.concatenate(outs, axis=0).T.astype(bf16)
 
-    if comm:
-
-        @pl.when(step == last)
-        def _():
-            gather.finish()
-            for s in swaps:
-                s.wait()
+
+def project_qkv(lanes, tok, cot, docs, norm_share, w, o, n, ff, comm):
+    t, d = tok.shape
+    rows = d // n
+    nb = d // 128
+    hs = ff // n // 2
+    r_in, r_bk = rows * ff // 128, ff // n * nb
+    at_in, at_bk = rows * 4 * nb, rows * 4 * nb + r_in
+    b_in, b_bk = r_in // UNPACK_STEPS, hs * nb // UNPACK_STEPS
+    assert at_in % b_in == 0 and at_bk % b_bk == 0
+    up = lambda i: jnp.minimum(i, UNPACK_STEPS - 1)
+    me = lambda: group_index(n)
+    whole = lambda s: pl.BlockSpec(s, lambda i: (0, 0))
+    half = 3 * d // 2
+    pairs, hd = d // 128, d // HEADS
+    per = 128 // hd
+    pair = lambda i: jnp.maximum(i - UNPACK_STEPS - 3, 0)
+    shapes = [sds((t, d), bf16), sds((t, 3 * d), bf16), sds((d, ff // 2), bf16), sds((ff // 2, d), bf16),
+              sds((d, half), bf16), sds((d, half), bf16), sds((d, d // 2), bf16), sds((d, d // 2), bf16), sds((4 * nb, 128), f32),
+              sds((t, d), bf16), sds((t, 1), jnp.int32), sds((t, d), bf16), sds((pairs, per, t), f32), sds((d, ff // 2), bf16),
+              sds((t, d), bf16), sds((t, d), bf16)]
+    w_args = [w, norm_share, o, norm_share] if comm else [w[0], w[1], o[0], o[1]]
+    outs = pl.pallas_call(
+        functools.partial(qkv_kernel, (n, comm, hd)),
+        grid=(UNPACK_STEPS + 3 + pairs,),
+        out_shape=shapes,
+        in_specs=[
+            ANY, whole(norm_share.shape),
+            pl.BlockSpec((b_in, 128), lambda i: (at_in // b_in + up(i), 0)),
+            pl.BlockSpec((b_bk, 128), lambda i: (at_bk // b_bk + lax.axis_index("core") * UNPACK_STEPS + up(i), 0)),
+            ANY, ANY, ANY, ANY, ANY, whole((1, t)),
+        ],
+        out_specs=[
+            ANY, ANY, ANY,
+            pl.BlockSpec((hs // UNPACK_STEPS, d), lambda i: (me() * UNPACK_STEPS + up(i), 0)),
+            ANY, ANY, ANY, ANY, whole((4 * nb, 128)), ANY, whole((t, 1)),
+            pl.BlockSpec((t, 128), lambda i: (0, pair(i))), pl.BlockSpec((1, per, t), lambda i: (pair(i), 0, 0)), ANY, ANY, ANY,
+        ],
+        scratch_shapes=[pltpu.VMEM((4 * nb, 128), f32), pltpu.VMEM((n, rows, 3 * d), bf16), pltpu.VMEM((t, d), bf16),
+                        pltpu.VMEM((t, 3 * d), f32), pltpu.VMEM((t, d), bf16), pltpu.VMEM((t, 3 * d), bf16), pltpu.VMEM((t, d), bf16),
+                        pltpu.VMEM((rows, ff // 2), bf16), pltpu.VMEM((t, t), f32), dma(6 + 2 * n), dma(38), dma(38)],
+        input_output_aliases={4: 4, 6: 6},
+        compiler_params=comm_params(1 if comm else None),
+        cost_estimate=cost(2 * t * d * 3 * d + 8 * t * t * d, 50e6, t * t * HEADS),
+        name="qkv_attend",
+    )(tok, norm_share, lanes, lanes, *w_args, cot, docs)
+    if comm:
+        return outs
+    full, oth = spread(outs[2])
+    return [*outs[:2], full, outs[3], w[0], w[1], o[0], o[1], *outs[8:13], oth, swap_core(outs[0]), swap_core(outs[9])]
+
+
+QB = 256
+
+
+def fill_bias(bias, doc_row, doc_col):
+    t = bias.shape[0]
+    for r in range(0, t, QB):
+        key = r + lax.broadcasted_iota(jnp.int32, (QB, t), 0)
+        query = lax.broadcasted_iota(jnp.int32, (QB, t), 1)
+        ok = (doc_col[r : r + QB, :] == doc_row[...]) & (key <= query)
+        bias[r : r + QB, :] = jnp.where(ok, 0.0, FILL)
+
+
+def head_lanes(v, h, hd):
+    lane = lax.broadcasted_iota(jnp.int32, v.shape, 1)
+    return jnp.where((lane >= h * hd) & (lane < (h + 1) * hd), v, jnp.zeros_like(v))
 
 
 def head_column(d, part):
     pairs = d // 256
     return lambda p: (0, (p // pairs) * 3 * pairs + part * pairs + p % pairs)
-
-
-def attend(qkv, doc_row, doc_col, w_own, a_one, d_out, d, comm):
-    t = qkv.shape[0]
-    pairs = d // 128
-    hd = d // HEADS
-    per = 128 // hd
-    col = lambda part: pl.BlockSpec((t, 128), head_column(d, part))
-    outs = pl.pallas_call(
-        functools.partial(attend_kernel, (hd, comm)),
-        grid=(pairs,),
-        out_shape=[sds((t, d), bf16), sds((pairs, per, t), f32), sds(w_own.shape, bf16), sds(w_own.shape, bf16),
-                   sds((t, d), bf16), sds((t, d), bf16)],
-        in_specs=[col(0), col(1), col(2), pl.BlockSpec((1, t), lambda p: (0, 0)), pl.BlockSpec((t, 1), lambda p: (0, 0)),
-                  ANY, ANY, ANY],
-        out_specs=[pl.BlockSpec((t, 128), lambda p: (0, p)), pl.BlockSpec((1, per, t), lambda p: (p, 0, 0)), ANY, ANY, ANY, ANY],
-        scratch_shapes=[pltpu.VMEM((t, t), f32), dma(13), dma(13)],
-        input_output_aliases={5: 2},
-        compiler_params=comm_params(2 if comm else None),
-        cost_estimate=cost(8 * t * t * d, 10e6, t * t * HEADS),
-        name="attend",
-    )(qkv, qkv, qkv, doc_row, doc_col, w_own, a_one, d_out)
-    if comm:
-        return outs
-    full, oth = spread(w_own)
-    return outs[0], outs[1], full, oth, swap_core(a_one), swap_core(d_out)
 
 
 def spread(own):
@@ -783,32 +780,32 @@
 FEED_PLAN = (
     (0, 1),
     (),
+    (),
     (10, 2),
+    (),
     (11, 3, 20),
-    (12, 4),
-    (21, 13, 5),
-    (22,),
-    (14, 6, 23),
-    (15, 7, 24),
-    (16,),
-    (25,),
-    (17, 26),
     (),
-    (27,),
+    (12, 4, 21),
     (),
+    (13, 5, 22),
+    (14, 6),
+    (23, 15, 7),
+    (24,),
+    (16, 25, 17),
+    (26, 27),
     (),
     (),
 )
 BACK_PLAN = (
-    (0, 1, 2),
+    (0, 1, 2, 3),
     (),
-    (10, 3, 11, 4, 30, 31),
-    (12, 5, 20, 32, 33, 40),
-    (13, 6, 21, 34, 35, 41, 42),
-    (14, 7, 22, 36, 37, 43, 44, 50),
-    (15, 23, 45, 51, 52, 16, 46),
-    (17, 24, 47, 53, 54, 25),
-    (26, 27, 55, 56, 57),
+    (30, 31, 10, 4, 11, 5),
+    (32, 40, 33, 12, 6),
+    (41, 20, 34, 13, 7, 42, 35),
+    (43, 21, 50, 36, 14, 15, 44, 37),
+    (45, 22, 51, 52, 16, 23, 46),
+    (47, 24, 53, 54, 17),
+    (25, 26, 27, 55, 56, 57),
 )
 LAST_PLAN = (
     (),
@@ -1019,12 +1016,13 @@
 
 
 def feed_kernel(comm, d_out, slope, b_own, b_oth, i_own, i_oth, resid, dout_rows, norms, o_own, o_oth, a_two, g_back, *refs):
-    (grad, d_resid, low, d_att, two_norm, sent, part_back, stage, theirs, lhs, dz, wo, lows, lsem, send, recv) = refs[:16]
+    (grad, d_resid, low, d_att, two_norm, sent, part_back, stage, theirs, lhs, wi, wo, lows, lsem, send, recv) = refs[:16]
     step = pl.program_id(0)
     nb = theirs.shape[0]
     tm, d = resid.shape
-    pro = dz.shape[0] // tm
+    pro = lows.shape[0] // tm
     half = d // 2
+    wide = wi.shape[1] // 2
     np_ = d // 128
     core = lax.axis_index("core")
     lo = pl.multiple_of(core * half, half)
@@ -1033,6 +1031,8 @@
         pltpu.make_async_copy(a_two, lhs.at[0], lsem.at[0]),
         pltpu.make_async_copy(o_own, wo.at[:, pl.ds(lo, half)], lsem.at[1]),
         pltpu.make_async_copy(o_oth, wo.at[:, pl.ds(hi, half)], lsem.at[2]),
+        pltpu.make_async_copy(i_oth, wi.at[:, pl.ds(0, wide)], lsem.at[4]),
+        pltpu.make_async_copy(i_own, wi.at[:, pl.ds(wide, wide)], lsem.at[5]),
     ]
 
     def hand(j):
@@ -1042,7 +1042,7 @@
         at = pl.ds(pl.multiple_of(r * tm, tm), tm)
         return hand_over(lows.at[at, :], sent.at[at, :], send.at[1 + nb + r], recv.at[1 + nb + r])
 
-    @pl.when(step == 0)
+    @pl.when(step == 1)
     def _():
         for cp in loads:
             cp.start()
@@ -1052,12 +1052,25 @@
         held, far, near, mid, total, keep = refs[16:22]
         scat = Scatter(g_back, held, far, near, mid, total, send, recv, 1 + nb + pro, part_back, keep)
         acts = (scat.begin, scat.turn, scat.close)
+        load = pltpu.make_async_copy(g_back, held, lsem.at[3])
+        near_by = [peer("core"), peer("x"), peer("y")]
 
         @pl.when(step == 0)
         def _():
-            load = pltpu.make_async_copy(g_back, held, lsem.at[3])
             load.start()
-            greet([peer("core"), peer("x"), peer("y")])
+            greet_start(near_by)
+
+    @pl.when(step < 2 * nb)
+    def _():
+        first = step < nb
+        g = (dot_nt(d_out[...], pick(first, b_oth[...], b_own[...])) * slope[...].astype(f32)).astype(bf16)
+        stage[step] = g
+
+    if comm:
+
+        @pl.when(step == 0)
+        def _():
+            greet_end(near_by)
             run_plan(acts, FEED_PLAN[0])
             swap.start()
             load.wait()
@@ -1069,21 +1082,6 @@
         @pl.when((step > 0) & (step <= nb))
         def _():
             hand(step - 1).start()
-
-    @pl.when(step < 2 * nb)
-    def _():
-        first = step < nb
-        g = (dot_nt(d_out[...], pick(first, b_oth[...], b_own[...])) * slope[...].astype(f32)).astype(bf16)
-        stage[step] = g
-        more = dot_nt(g, pick(first, i_oth[...], i_own[...]))
-
-        @pl.when(step == 0)
-        def _():
-            dz[...] = more
-
-        @pl.when(step > 0)
-        def _():
-            dz[...] += more
 
     @pl.when(step == 2 * nb)
     def _():
@@ -1108,14 +1106,15 @@
 
     @pl.when(step == 3 * nb)
     def _():
-        loads[1].wait()
-        loads[2].wait()
+        for cp in loads[1:]:
+            cp.wait()
         two_norm[...] = jnp.zeros_like(two_norm)
 
     @pl.when(step >= 3 * nb)
     def _():
         here = pl.ds(pl.multiple_of((step - 3 * nb) * tm, tm), tm)
-        dv, g, b = layer_norm_back(resid[...], gain_row(norms, 2, d), dz[here, :])
+        dz = dot_nt(jnp.concatenate([stage[j, here, :] for j in range(2 * nb)], axis=1), wi[...])
+        dv, g, b = layer_norm_back(resid[...], gain_row(norms, 2, d), dz)
         two_norm[0:np_, :] += flat_row(g)
         two_norm[np_:, :] += flat_row(b)
         dr = dout_rows[...].astype(f32) + dv
@@ -1160,12 +1159,11 @@
                    sds((t, d // 2), bf16), sds(part, bf16)],
         in_specs=[whole((t, d)), pl.BlockSpec((t, blk), lambda i: (0, jnp.where(i < nb, nb + i, own(i)))),
                   pl.BlockSpec((blk, d), lambda i: (own(i), 0)), pl.BlockSpec((blk, d), lambda i: (oth(i), 0)),
-                  pl.BlockSpec((d, blk), lambda i: (0, own(i))), pl.BlockSpec((d, blk), lambda i: (0, oth(i))),
-                  rows(d), rows(d), whole(norms.shape), ANY, ANY, ANY, ANY],
+                  ANY, ANY, rows(d), rows(d), whole(norms.shape), ANY, ANY, ANY, ANY],
         out_specs=[pl.BlockSpec((blk // per, d, per), lambda i: (jnp.clip(i - 2 * nb, 0, nb - 1), 0, 0)), rows(d), rows(d), rows(d),
                    whole((d // 64, 128)), ANY, ANY],
         scratch_shapes=[pltpu.VMEM((2 * nb, t, blk), bf16), pltpu.VMEM((nb, t, blk), bf16), pltpu.VMEM((2, t, d), bf16),
-                        pltpu.VMEM((t, d), f32), pltpu.VMEM((d, d), bf16), pltpu.VMEM((t, d // 2), bf16), dma(4), dma(sems), dma(sems)]
+                        pltpu.VMEM((d, 2 * half), bf16), pltpu.VMEM((d, d), bf16), pltpu.VMEM((t, d // 2), bf16), dma(6), dma(sems), dma(sems)]
         + extra,
         compiler_params=comm_params(4 if comm else None, 62),
         cost_estimate=cost(12 * t * d * half + 2 * t * d * d, 60e6),
@@ -1267,7 +1265,7 @@
 
     @pl.when(step == 0)
     def _():
-        for cp in early + mids:
+        for cp in early:
             cp.start()
         if comm:
             load = pltpu.make_async_copy(part_in, mine_in, lsem.at[8])
@@ -1276,8 +1274,10 @@
             for s in range(PIECES):
                 fold_in.begin(s)
             load.wait()
-        for cp in early:
+        for cp in early[:2]:
             cp.wait()
+        for cp in mids:
+            cp.start()
         parts[0 : 2 * nb, :] = jnp.zeros((2 * nb, 128), f32)
         parts[2 * nb :, :] = two_norm[...]
 
@@ -1293,6 +1293,11 @@
         g = pick(step < per, g1[...], pick(step < 2 * per, g2[...], g3[...]))
         acc = dot_tn(wb[0:d, :], g) + dot_tn(wb[d : 2 * d, :], theirs[...])
         held[step] = acc.astype(bf16)
+
+    @pl.when(step == 3 * per)
+    def _():
+        for cp in early[2:]:
+            cp.wait()
 
     @pl.when((step >= 3 * per) & (step < np_))
     def _():
@@ -1510,7 +1515,6 @@
     inv_root, at_in, at_at, counts = cfg
     step = pl.program_id(0)
     core = lax.axis_index("core")
-    first = core == 0
     n_back, n_in, n_at = counts
 
     @pl.when(step < n_back)
@@ -1526,10 +1530,9 @@
         rows, wide = own.shape[1:]
         for col, lo, hi, stride in places:
             p, c = col // wide, col % wide
-            a = own[p, :, c : c + 128].astype(f32) * inv_root
-            b = oth[p, :, c : c + 128].astype(f32) * inv_root
-            dst[pl.ds(lo, rows, stride=stride), :] = pick(first, a, b)
-            dst[pl.ds(hi, rows, stride=stride), :] = pick(first, b, a)
+            mine = lo + core * (hi - lo)
+            dst[pl.ds(mine, rows, stride=stride), :] = own[p, :, c : c + 128].astype(f32) * inv_root
+            dst[pl.ds(lo + hi - mine, rows, stride=stride), :] = oth[p, :, c : c + 128].astype(f32) * inv_root
 
     @pl.when((step >= n_back) & (step < n_back + n_in))
     def _():
@@ -1612,10 +1615,9 @@
         w, o = spread(w), spread(o)
         norm_share = lax.all_gather(master[-(4 * d // n) :].astype(bf16), ("y", "x"), axis=0, tiled=True)
         norm_share = norm_share.astype(f32).reshape(-1, 128)
-    a_one, qkv, in_own, bk_own, w_own, w_oth, o_own, o_oth, norms, d_out, doc_col = project_qkv(
+    (a_one, qkv, in_own, bk_own, w_own, w_oth, o_own, o_oth, norms, d_out, doc_col, att, lse, in_oth, a_one_p, d_out_p) = project_qkv(
         lanes, tokens, cotangent, doc_row, norm_share, w, o, n, ff, comm
     )
-    att, lse, in_own, in_oth, a_one_p, d_out_p = attend(qkv, doc_row, doc_col, in_own, a_one, d_out, d, comm)
     resid, a_two, hidden, slope, bk_own, bk_oth, att_p, g_back = middle(
         att, tokens, norms, o_own, o_oth, in_own, in_oth, bk_own, d_out, d_out_p, comm
     )

time: 347 us -> 341 us (0.983)
  Pallas kernels: 342 us -> 336 us
    pallas_call x2 -> x1, Pallas kernels: 85.8 us -> 82.2 us  [project_qkv(): pl.pallas_call(functools.partial(qkv_kernel, (n, comm, hd)), grid=(UNPACK...]
where the time goes in v2:
time: 341 us; the launch traced here: 340 us
  Pallas kernels  336 us (99%)
  local copies, waits for them, and re-layouts  3.65 us (1%)
    pallas_call x1, Pallas kernels, project_qkv(): pl.pallas_call(functools.partial(qkv_kernel, (n, comm, hd)), grid=(UNPACK...  82.2 us
    pallas_call x1, Pallas kernels, last_grad(): pl.pallas_call(functools.partial(last_kernel, (d, comm)), grid=(np_ + 2 *...  72.2 us
    pallas_call x1, Pallas kernels, feed_back(): pl.pallas_call(functools.partial(feed_kernel, comm), grid=(3 * nb + pro,)...  56.6 us
    pallas_call x1, Pallas kernels, attend_back(): pl.pallas_call(functools.partial(attend_back_kernel, (hd, comm)), grid=(p...  48.2 us
    pallas_call x1, Pallas kernels, middle(): pl.pallas_call(functools.partial(middle_kernel, (d, tm, blk, comm)), grid...  44.4 us
    pallas_call x1, Pallas kernels, adam_all(): pl.pallas_call(functools.partial(adam_all_kernel, cfg), grid=(n_back + n_...  27.9 us

profile of v2, /device:TPU:0, one launch (start us, length us, event | category | flops | bytes accessed | tf_op | source)
XLA Modules:
  0.0 339.9 jit_solution(1365356794005059544)
XLA Ops:
  0.6 4.1 %unpack.1 = (bf16[1024,1536]{1,0:T(8,128)(2,1)}, bf16[1024,512]{1,0:T(8,128)(2,1)}, f32[8,128]{1,0:T(8,128)}) custom-call(f32[24584,128]{1,0:T(8,128)} %bitcast.7, f32[24584,128]{1,0:T(8,128)} %bitcast.8, f32[24584,128]{1,0:T(8,128)} %bitcast.9), custom_call_target="tpu_custom_call" | custom-call | tf_op jit(solution)/shard_map/unpack/pallas_call | solution.py:361
  4.8 82.2 %qkv_attend.1 = (bf16[1024,1024]{1,0:T(8,128)(2,1)}, bf16[1024,3072]{1,0:T(8,128)(2,1)}, bf16[1024,2048]{1,0:T(8,128)(2,1)}, bf16[2048,1024]{1,0:T(8,128)(2,1)},...) custom-call(bf16[1024,1024]{1,0:T(8,128)(2,1)} %tok.5, ...), custom_call_target="tpu_custom_call", output_to_operand_aliasing={{4}: (4, {}), {6}: (6, {})} | custom-call | flops 15032385536 | bytes 50000000 | tf_op jit(solution)/shard_map/qkv_attend/pallas_call | solution.py:624
  87.0 44.4 %middle.1 = (f32[1024,1024]{1,0:T(8,128)}, bf16[1024,1024]{1,0:T(8,128)(2,1)}, bf16[1024,4096]{1,0:T(8,128)(2,1)}, bf16[1024,4096]{1,0:T(8,128)(2,1)}, bf16[2048...) custom-call(bf16[1024,1024]{1,0:T(8,128)(2,1)} %get-tuple-element.61, ...), custom_call_target="tpu_custom_call", output_to_operand_aliasing={{4}: (8, {})} | custom-call | flops 19327352832 | bytes 60000000 | tf_op jit(solution)/shard_map/middle/pallas_call | solution.py:989
  131.4 56.6 %feed_back.1 = (bf16[8,1024,256]{2,1,0:T(8,128)(2,1)}, f32[1024,1024]{1,0:T(8,128)}, bf16[1024,1024]{1,0:T(8,128)(2,1)}, bf16[1024,1024]{1,0:T(8,128)(2,1)}, f32...) custom-call(bf16[1024,1024]{1,0:T(8,128)(2,1)} %get-tuple-element.60.d_out.dout_rows, ...), custom_call_target="tpu_custom_call" | custom-call | flops 27917287424 | bytes 60000000 | tf_op jit(solution)/shard_map/feed_back/pallas_call | solution.py:1155
  188.0 48.2 %attend_back.1 = (bf16[1024,1024]{1,0:T(8,128)(2,1)}, bf16[1024,1024]{1,0:T(8,128)(2,1)}, bf16[1024,1024]{1,0:T(8,128)(2,1)}, bf16[1024,1536]{1,0:T(8,128)(2,1)}...) custom-call(bf16[1024,3072]{1,0:T(8,128)(2,1)} %get-tuple-element.59.q.k.v, ...), custom_call_target="tpu_custom_call" | custom-call | flops 21474836480 | bytes 16000000 | tf_op jit(solution)/shard_map/attend_back/pallas_call | solution.py:847
  236.2 72.2 %last_grad.1 = (bf16[1024,1024]{1,0:T(8,128)(2,1)}, bf16[1024,1024]{1,0:T(8,128)(2,1)}, bf16[8,256,256]{2,1,0:T(8,128)(2,1)}, bf16[8,256,256]{2,1,0:T(8,128)(2,1...) custom-call(bf16[1024,1024]{1,0:T(8,128)(2,1)} %get-tuple-element.80.g1.dq, ...), custom_call_target="tpu_custom_call" | custom-call | flops 23622320128 | bytes 60000000 | tf_op jit(solution)/shard_map/last_grad/pallas_call | solution.py:1398
  308.3 0.0 copy-start.1
  308.4 27.9 %adam_all.1 = (f32[24584,128]{1,0:T(8,128)}, f32[24584,128]{1,0:T(8,128)}, f32[24584,128]{1,0:T(8,128)}) custom-call(bf16[8,512,128]{2,1,0:T(8,128)(2,1)} %get-tuple-element.97.b_own, bf16[8,512,128]{2,1,0:T(8,128)(2,1)} %get-tuple-element.98.b_oth, bf16[8,256,256]{2,1,0:T(8,128)(2,1)} %get-tuple-element.99.i_own, ...), custom_call_target="tpu_custom_call" | custom-call | bytes 69228544 | tf_op jit(solution)/shard_map/adam_all/pallas_call | solution.py:1587
  336.2 0.0 copy-start
  336.2 0.0 copy-done.1
  336.3 1.3 copy.19
  337.6 1.0 copy-done
  338.6 1.3 copy.20
Async XLA Ops:
  308.3 27.9 %copy-start.1 = (bf16[1024,1024]{1,0:T(8,128)(2,1)S(1)}, bf16[1024,1024]{1,0:T(8,128)(2,1)}, u32[]{:S(2)}) copy-start(bf16[1024,1024]{1,0:T(8,128)(2,1)} %get-tuple-element.112) | copy-start | bytes 6291460
  336.2 2.3 copy-start

commit v3 on v2

--- a/solution.py
+++ b/solution.py
@@ -383,7 +383,7 @@
 def qkv_kernel(cfg, tok, norm_share, m_in, m_back, w_own_in, w_oth_in, o_own_in, o_oth_in, cot, docs, *refs):
     n, comm, hd = cfg
     (a_hbm, qkv_hbm, in_own, own_bk, w_own, w_oth, o_own, o_oth, norms_out, d_hbm, doc_col, att, lse, in_oth, a_p, d_p,
-     norms, w, toks, acc, cots, qkv, a_out, own_in, bias, lsem, send, recv) = refs
+     norms, w, toks, acc, cots, qkv, a_out, own_in, bias, raw, own_w, own_o, noted, lsem, send, recv) = refs
     if not comm:
         w_own, w_oth = w_own_in, w_oth_in
     t, d = toks.shape
@@ -398,6 +398,11 @@
     d_copy = pltpu.make_async_copy(cots, d_hbm, lsem.at[3 + 2 * n])
     place = pl.ds(pl.multiple_of(group_index(n) * share, 8), share)
     in_copy = pltpu.make_async_copy(own_in, in_own.at[place, :], lsem.at[5 + 2 * n])
+    if comm:
+        own_copies = [
+            pltpu.make_async_copy(own_w, w_own.at[place, :], lsem.at[7 + 2 * n]),
+            pltpu.make_async_copy(own_o, o_own.at[place, :], lsem.at[8 + 2 * n]),
+        ]
     out = pltpu.make_async_copy(qkv, qkv_hbm, lsem.at[4 + 2 * n])
 
     if comm:
@@ -406,13 +411,13 @@
         mine = pl.ds(pl.multiple_of(me * 8, 8), 8)
         notes = [
             pltpu.make_async_remote_copy(
-                src_ref=norm_share, dst_ref=norms.at[mine, :], send_sem=send.at[22 + i], recv_sem=recv.at[22 + i],
+                src_ref=noted, dst_ref=norms.at[mine, :], send_sem=send.at[22 + i], recv_sem=recv.at[22 + i],
                 device_id=p, device_id_type=MESH,
             )
             for i, p in enumerate(near)
         ]
-        first = Gather(w_own, w_oth, send, recv, 0)
-        second = Gather(o_own, o_oth, send, recv, 11)
+        first = Gather(w_own, w_oth, send, recv, 0, own_w)
+        second = Gather(o_own, o_oth, send, recv, 11, own_o)
         third = Gather(in_own, in_oth, send, recv, 25, own_in)
         swaps = [hand_over(a_out, a_p, send.at[36], recv.at[36]), hand_over(cots, d_p, send.at[37], recv.at[37])]
         rows = first.rows
@@ -424,11 +429,31 @@
         tok_copy.start()
         cot_copy.start()
         if comm:
-            greet(near + [peer("core")])
+            fetch = pltpu.make_async_copy(w_own_in.at[pl.ds(0, raw.shape[0]), :], raw, lsem.at[6 + 2 * n])
+            fetch.start()
+            greet_start(near + [peer("core")])
+            noted[...] = norm_share[...].astype(bf16).astype(f32)
+            norms[mine, :] = noted[...]
+            fetch.wait()
+            core = lax.axis_index("core")
+            hb = nb // 2
+
+            @pl.loop(0, hb)
+            def _(c):
+                def put(base, own, dst, lo, stride):
+                    cols = pl.ds(pl.multiple_of((dst + c) * 128, 128), 128)
+                    own[:, cols] = raw[pl.ds(base + lo + c + core * hb, share, stride=stride), :].astype(bf16)
+
+                for part in range(3):
+                    put(0, own_w, part * hb, part * nb, 3 * nb)
+                put(share * 3 * nb, own_o, 0, 0, nb)
+
+            greet_end(near + [peer("core")])
             for m in notes:
                 m.start()
             first.begin()
-            norms[mine, :] = norm_share[...]
+            own_copies[0].start()
+            own_copies[1].start()
 
     @pl.when(step < UNPACK_STEPS)
     def _():
@@ -498,6 +523,7 @@
         in_copy.start()
         fill_bias(bias, docs, doc_col)
         if comm:
+            own_copies[0].wait()
             first.arrive(4)
         load(0)
 
@@ -570,6 +596,7 @@
     @pl.when(step == pl.num_programs(0) - 1)
     def _():
         if comm:
+            own_copies[1].wait()
             third.finish()
             second.arrive(4, 7, 8, 9, 10)
             second.sent()
@@ -620,13 +647,18 @@
               sds((d, half), bf16), sds((d, half), bf16), sds((d, d // 2), bf16), sds((d, d // 2), bf16), sds((4 * nb, 128), f32),
               sds((t, d), bf16), sds((t, 1), jnp.int32), sds((t, d), bf16), sds((pairs, per, t), f32), sds((d, ff // 2), bf16),
               sds((t, d), bf16), sds((t, d), bf16)]
-    w_args = [w, norm_share, o, norm_share] if comm else [w[0], w[1], o[0], o[1]]
+    w_args = [lanes] * 4 if comm else [w[0], w[1], o[0], o[1]]
+    if comm:
+        norm_share = lanes
+        norm_spec = pl.BlockSpec((8, 128), lambda i: (lanes.shape[0] // 8 - 1, 0))
+    else:
+        norm_spec = whole(norm_share.shape)
     outs = pl.pallas_call(
         functools.partial(qkv_kernel, (n, comm, hd)),
         grid=(UNPACK_STEPS + 3 + pairs,),
         out_shape=shapes,
         in_specs=[
-            ANY, whole(norm_share.shape),
+            ANY, norm_spec,
             pl.BlockSpec((b_in, 128), lambda i: (at_in // b_in + up(i), 0)),
             pl.BlockSpec((b_bk, 128), lambda i: (at_bk // b_bk + lax.axis_index("core") * UNPACK_STEPS + up(i), 0)),
             ANY, ANY, ANY, ANY, ANY, whole((1, t)),
@@ -639,8 +671,10 @@
         ],
         scratch_shapes=[pltpu.VMEM((4 * nb, 128), f32), pltpu.VMEM((n, rows, 3 * d), bf16), pltpu.VMEM((t, d), bf16),
                         pltpu.VMEM((t, 3 * d), f32), pltpu.VMEM((t, d), bf16), pltpu.VMEM((t, 3 * d), bf16), pltpu.VMEM((t, d), bf16),
-                        pltpu.VMEM((rows, ff // 2), bf16), pltpu.VMEM((t, t), f32), dma(6 + 2 * n), dma(38), dma(38)],
-        input_output_aliases={4: 4, 6: 6},
+                        pltpu.VMEM((rows, ff // 2), bf16), pltpu.VMEM((t, t), f32), pltpu.VMEM((rows * 4 * nb, 128), f32),
+                        pltpu.VMEM((rows, half), bf16), pltpu.VMEM((rows, d // 2), bf16), pltpu.VMEM((8, 128), f32),
+                        dma(9 + 2 * n), dma(38), dma(38)],
+        input_output_aliases={} if comm else {4: 4, 6: 6},
         compiler_params=comm_params(1 if comm else None),
         cost_estimate=cost(2 * t * d * 3 * d + 8 * t * t * d, 50e6, t * t * HEADS),
         name="qkv_attend",
@@ -1609,9 +1643,10 @@
     comm = n == 4 and nz == 4
 
     lanes = master.reshape(-1, 128)
-    w, o, norm_share = unpack_first(lanes, n, d, ff)
     doc_row = doc_ids.reshape(1, t)
+    w = o = norm_share = None
     if not comm:
+        w, o, _ = unpack_first(lanes, n, d, ff)
         w, o = spread(w), spread(o)
         norm_share = lax.all_gather(master[-(4 * d // n) :].astype(bf16), ("y", "x"), axis=0, tiled=True)
         norm_share = norm_share.astype(f32).reshape(-1, 128)

time: 341 us -> 339 us (level)
    pallas_call x1 -> x0, Pallas kernels: 4.12 us -> none  [unpack_first(): pl.pallas_call(functools.partial(unpack_kernel, (n, d)), grid=(steps,), o...]
where the time goes in v3:
time: 339 us; the launch traced here: 338 us
  Pallas kernels  334 us (99%)
  local copies, waits for them, and re-layouts  3.65 us (1%)
    pallas_call x1, Pallas kernels, project_qkv(): pl.pallas_call(functools.partial(qkv_kernel, (n, comm, hd)), grid=(UNPACK...  84.8 us
    pallas_call x1, Pallas kernels, last_grad(): pl.pallas_call(functools.partial(last_kernel, (d, comm)), grid=(np_ + 2 *...  72.1 us
    pallas_call x1, Pallas kernels, feed_back(): pl.pallas_call(functools.partial(feed_kernel, comm), grid=(3 * nb + pro,)...  56.7 us
    pallas_call x1, Pallas kernels, attend_back(): pl.pallas_call(functools.partial(attend_back_kernel, (hd, comm)), grid=(p...  48.1 us
    pallas_call x1, Pallas kernels, middle(): pl.pallas_call(functools.partial(middle_kernel, (d, tm, blk, comm)), grid...  44.4 us
    pallas_call x1, Pallas kernels, adam_all(): pl.pallas_call(functools.partial(adam_all_kernel, cfg), grid=(n_back + n_...  27.9 us

profile of v3, /device:TPU:0, one launch (start us, length us, event | category | flops | bytes accessed | tf_op | source)
XLA Modules:
  0.0 338.5 jit_solution(14007210708461607309)
XLA Ops:
  0.6 84.8 %qkv_attend.1 = (bf16[1024,1024]{1,0:T(8,128)(2,1)}, bf16[1024,3072]{1,0:T(8,128)(2,1)}, bf16[1024,2048]{1,0:T(8,128)(2,1)}, bf16[2048,1024]{1,0:T(8,128)(2,1)},...) custom-call(bf16[1024,1024]{1,0:T(8,128)(2,1)} %tok.5, ...), custom_call_target="tpu_custom_call" | custom-call | flops 15032385536 | bytes 50000000 | tf_op jit(solution)/shard_map/qkv_attend/pallas_call | solution.py:656
  85.5 44.4 %middle.1 = (f32[1024,1024]{1,0:T(8,128)}, bf16[1024,1024]{1,0:T(8,128)(2,1)}, bf16[1024,4096]{1,0:T(8,128)(2,1)}, bf16[1024,4096]{1,0:T(8,128)(2,1)}, bf16[2048...) custom-call(bf16[1024,1024]{1,0:T(8,128)(2,1)} %get-tuple-element.55, ...), custom_call_target="tpu_custom_call", output_to_operand_aliasing={{4}: (8, {})} | custom-call | flops 19327352832 | bytes 60000000 | tf_op jit(solution)/shard_map/middle/pallas_call | solution.py:1023
  129.9 56.7 %feed_back.1 = (bf16[8,1024,256]{2,1,0:T(8,128)(2,1)}, f32[1024,1024]{1,0:T(8,128)}, bf16[1024,1024]{1,0:T(8,128)(2,1)}, bf16[1024,1024]{1,0:T(8,128)(2,1)}, f32...) custom-call(bf16[1024,1024]{1,0:T(8,128)(2,1)} %get-tuple-element.54.d_out.dout_rows, ...), custom_call_target="tpu_custom_call" | custom-call | flops 27917287424 | bytes 60000000 | tf_op jit(solution)/shard_map/feed_back/pallas_call | solution.py:1189
  186.6 48.1 %attend_back.1 = (bf16[1024,1024]{1,0:T(8,128)(2,1)}, bf16[1024,1024]{1,0:T(8,128)(2,1)}, bf16[1024,1024]{1,0:T(8,128)(2,1)}, bf16[1024,1536]{1,0:T(8,128)(2,1)}...) custom-call(bf16[1024,3072]{1,0:T(8,128)(2,1)} %get-tuple-element.53.q.k.v, ...), custom_call_target="tpu_custom_call" | custom-call | flops 21474836480 | bytes 16000000 | tf_op jit(solution)/shard_map/attend_back/pallas_call | solution.py:881
  234.7 72.1 %last_grad.1 = (bf16[1024,1024]{1,0:T(8,128)(2,1)}, bf16[1024,1024]{1,0:T(8,128)(2,1)}, bf16[8,256,256]{2,1,0:T(8,128)(2,1)}, bf16[8,256,256]{2,1,0:T(8,128)(2,1...) custom-call(bf16[1024,1024]{1,0:T(8,128)(2,1)} %get-tuple-element.74.g1.dq, ...), custom_call_target="tpu_custom_call" | custom-call | flops 23622320128 | bytes 60000000 | tf_op jit(solution)/shard_map/last_grad/pallas_call | solution.py:1432
  306.9 0.0 copy-start.1
  306.9 27.9 %adam_all.1 = (f32[24584,128]{1,0:T(8,128)}, f32[24584,128]{1,0:T(8,128)}, f32[24584,128]{1,0:T(8,128)}) custom-call(bf16[8,512,128]{2,1,0:T(8,128)(2,1)} %get-tuple-element.91.b_own, bf16[8,512,128]{2,1,0:T(8,128)(2,1)} %get-tuple-element.92.b_oth, bf16[8,256,256]{2,1,0:T(8,128)(2,1)} %get-tuple-element.93.i_own, ...), custom_call_target="tpu_custom_call" | custom-call | bytes 69228544 | tf_op jit(solution)/shard_map/adam_all/pallas_call | solution.py:1621
  334.8 0.0 copy-start
  334.8 0.0 copy-done.1
  334.8 1.3 copy.15
  336.1 1.0 copy-done
  337.1 1.3 copy.16
Async XLA Ops:
  306.9 27.9 %copy-start.1 = (bf16[1024,1024]{1,0:T(8,128)(2,1)S(1)}, bf16[1024,1024]{1,0:T(8,128)(2,1)}, u32[]{:S(2)}) copy-start(bf16[1024,1024]{1,0:T(8,128)(2,1)} %get-tuple-element.106) | copy-start | bytes 6291460
  334.8 2.3 copy-start

commit v4 on v3

--- a/solution.py
+++ b/solution.py
@@ -582,6 +582,10 @@
             third.forward()
             second.close()
 
+        @pl.when(step == start + 7)
+        def _():
+            third.close()
+
     @pl.when(step >= start)
     def _():
         pair = step - start
@@ -597,7 +601,8 @@
     def _():
         if comm:
             own_copies[1].wait()
-            third.finish()
+            third.arrive(4, 7, 8, 9, 10)
+            third.sent()
             second.arrive(4, 7, 8, 9, 10)
             second.sent()
             first.sent()
@@ -986,6 +991,10 @@
         def _():
             gather.forward()
 
+        @pl.when(step == last)
+        def _():
+            gather.close()
+
     @pl.when(step >= pro + 2 * nb)
     def _():
         j = step - pro - 2 * nb
@@ -998,7 +1007,8 @@
 
         @pl.when(step == last)
         def _():
-            gather.finish()
+            gather.arrive(4, 7, 8, 9, 10)
+            gather.sent()
             swap.wait()
             for j in range(nb):
                 hand(j).wait_send()

time: 339 us -> 335 us (0.988)
  Pallas kernels: 334 us -> 330 us
where the time goes in v4:
time: 335 us
  Pallas kernels  330 us (99%)
  local copies, waits for them, and re-layouts  3.65 us (1%)
    pallas_call x1, Pallas kernels, project_qkv(): pl.pallas_call(functools.partial(qkv_kernel, (n, comm, hd)), grid=(UNPACK...  82.7 us
    pallas_call x1, Pallas kernels, last_grad(): pl.pallas_call(functools.partial(last_kernel, (d, comm)), grid=(np_ + 2 *...  71.9 us
    pallas_call x1, Pallas kernels, feed_back(): pl.pallas_call(functools.partial(feed_kernel, comm), grid=(3 * nb + pro,)...  55.4 us
    pallas_call x1, Pallas kernels, attend_back(): pl.pallas_call(functools.partial(attend_back_kernel, (hd, comm)), grid=(p...  48.2 us
    pallas_call x1, Pallas kernels, middle(): pl.pallas_call(functools.partial(middle_kernel, (d, tm, blk, comm)), grid...  44.3 us
    pallas_call x1, Pallas kernels, adam_all(): pl.pallas_call(functools.partial(adam_all_kernel, cfg), grid=(n_back + n_...  27.9 us

profile of v4, /device:TPU:0, one launch (start us, length us, event | category | flops | bytes accessed | tf_op | source)
XLA Modules:
  0.0 334.7 jit_solution(5506868275483188052)
XLA Ops:
  0.6 82.7 %qkv_attend.1 = (bf16[1024,1024]{1,0:T(8,128)(2,1)}, bf16[1024,3072]{1,0:T(8,128)(2,1)}, bf16[1024,2048]{1,0:T(8,128)(2,1)}, bf16[2048,1024]{1,0:T(8,128)(2,1)},...) custom-call(bf16[1024,1024]{1,0:T(8,128)(2,1)} %tok.5, ...), custom_call_target="tpu_custom_call" | custom-call | flops 15032385536 | bytes 50000000 | tf_op jit(solution)/shard_map/qkv_attend/pallas_call | solution.py:661
  83.3 44.3 %middle.1 = (f32[1024,1024]{1,0:T(8,128)}, bf16[1024,1024]{1,0:T(8,128)(2,1)}, bf16[1024,4096]{1,0:T(8,128)(2,1)}, bf16[1024,4096]{1,0:T(8,128)(2,1)}, bf16[2048...) custom-call(bf16[1024,1024]{1,0:T(8,128)(2,1)} %get-tuple-element.55, ...), custom_call_target="tpu_custom_call", output_to_operand_aliasing={{4}: (8, {})} | custom-call | flops 19327352832 | bytes 60000000 | tf_op jit(solution)/shard_map/middle/pallas_call | solution.py:1033
  127.6 55.4 %feed_back.1 = (bf16[8,1024,256]{2,1,0:T(8,128)(2,1)}, f32[1024,1024]{1,0:T(8,128)}, bf16[1024,1024]{1,0:T(8,128)(2,1)}, bf16[1024,1024]{1,0:T(8,128)(2,1)}, f32...) custom-call(bf16[1024,1024]{1,0:T(8,128)(2,1)} %get-tuple-element.54.d_out.dout_rows, ...), custom_call_target="tpu_custom_call" | custom-call | flops 27917287424 | bytes 60000000 | tf_op jit(solution)/shard_map/feed_back/pallas_call | solution.py:1199
  183.0 48.2 %attend_back.1 = (bf16[1024,1024]{1,0:T(8,128)(2,1)}, bf16[1024,1024]{1,0:T(8,128)(2,1)}, bf16[1024,1024]{1,0:T(8,128)(2,1)}, bf16[1024,1536]{1,0:T(8,128)(2,1)}...) custom-call(bf16[1024,3072]{1,0:T(8,128)(2,1)} %get-tuple-element.53.q.k.v, ...), custom_call_target="tpu_custom_call" | custom-call | flops 21474836480 | bytes 16000000 | tf_op jit(solution)/shard_map/attend_back/pallas_call | solution.py:886
  231.2 71.9 %last_grad.1 = (bf16[1024,1024]{1,0:T(8,128)(2,1)}, bf16[1024,1024]{1,0:T(8,128)(2,1)}, bf16[8,256,256]{2,1,0:T(8,128)(2,1)}, bf16[8,256,256]{2,1,0:T(8,128)(2,1...) custom-call(bf16[1024,1024]{1,0:T(8,128)(2,1)} %get-tuple-element.74.g1.dq, ...), custom_call_target="tpu_custom_call" | custom-call | flops 23622320128 | bytes 60000000 | tf_op jit(solution)/shard_map/last_grad/pallas_call | solution.py:1442
  303.1 0.0 copy-start.1
  303.1 27.9 %adam_all.1 = (f32[24584,128]{1,0:T(8,128)}, f32[24584,128]{1,0:T(8,128)}, f32[24584,128]{1,0:T(8,128)}) custom-call(bf16[8,512,128]{2,1,0:T(8,128)(2,1)} %get-tuple-element.91.b_own, bf16[8,512,128]{2,1,0:T(8,128)(2,1)} %get-tuple-element.92.b_oth, bf16[8,256,256]{2,1,0:T(8,128)(2,1)} %get-tuple-element.93.i_own, ...), custom_call_target="tpu_custom_call" | custom-call | bytes 69228544 | tf_op jit(solution)/shard_map/adam_all/pallas_call | solution.py:1631
  331.0 0.0 copy-start
  331.0 0.0 copy-done.1
  331.0 1.3 copy.15
  332.3 1.0 copy-done
  333.3 1.3 copy.16
Async XLA Ops:
  303.1 27.9 %copy-start.1 = (bf16[1024,1024]{1,0:T(8,128)(2,1)S(1)}, bf16[1024,1024]{1,0:T(8,128)(2,1)}, u32[]{:S(2)}) copy-start(bf16[1024,1024]{1,0:T(8,128)(2,1)} %get-tuple-element.106) | copy-start | bytes 6291460
  331.0 2.3 copy-start
